TPU v7x, 32 devices: a whole 2x2x4 slice. The times are simulated.
32 devices in a mesh: grp: 8 (over z, y), dir: 4 (over x, core).
Axes of the slice: x: 2, y: 2, z: 4, core: 2. Of those that a mesh axis runs over, the one named last changes fastest.
Arguments:
- currents: bfloat16 [2048, 128], P('grp'), may hold values from -6 to 6
- basis_group: int32 [2048], P('grp'), may hold values from 0 to 1
- projection: bfloat16 [2048, 1024], P('grp', 'dir'), may hold values from -0.5 to 0.5
- filters: bfloat16 [4, 64, 1024], P(None, None, 'dir'), may hold values from -0.25 to 0.25
- pair_src: int32 [128], P('grp'), may hold values from 0 to 7, as said below
- pair_dst: int32 [128], P('grp'), may hold values from 0 to 7, as said below
- pair_type: int32 [128], P('grp'), may hold values from 0 to 3
- live_count: int32 [8], P('grp'), may hold values from 8 to 16, as said below
- send_group: int32 [8, 8], replicated, may hold values from 0 to 1, as said below
- recv_group: int32 [8, 8], replicated, may hold values from 0 to 1, as said below
Outputs:
- field: bfloat16 [2048, 128], P('grp')
Inputs may be any that keep to these rules, and one draw needn't show every extreme that they name: `pair_src`: for each reader, its first 8 slots name every owner once. `pair_dst`: for each reader, its first 8 slots name every owner once. `live_count`: some reader has all 16 slots live. `send_group`: each row names every one of the owner's groups at least once. `recv_group`: each row names every one of the owner's groups at least once.
All inputs are finite; a program needn't handle non-finite values.
Results may differ from a plain program's by a relative error of at most 0.0058.
Values may be sent and summed in bfloat16 or wider, within the bound.
No kernel may reach another device: no remote copies, remote signals or barrier semaphores. Data moves between devices by JAX's collectives and lax.ppermute only.
A program may use at most 192 MiB of HBM per device.

v0:
```python
import math

import jax
import jax.numpy as jnp
from jax import lax
from jax.sharding import PartitionSpec as P

TAPS = 64
G_DEV = 2
TYPES = 4


def local(
    currents,
    basis_group,
    projection,
    filters,
    pair_src,
    pair_dst,
    pair_type,
    live_count,
    send_group,
    recv_group,
):
    readers = lax.axis_size("grp")
    position = lax.axis_index("grp")
    steps = currents.shape[1]
    width = projection.shape[1]
    slots = pair_src.shape[0]
    labels = jnp.arange(G_DEV, dtype=jnp.int32)
    member = (basis_group[:, None] == labels[None, :]).astype(jnp.bfloat16)
    spread = currents[:, None, :] * member[:, :, None]
    signature = jnp.einsum(
        "bk,bgt->gkt", projection, spread, preferred_element_type=jnp.float32
    ).astype(jnp.bfloat16)
    own_row = lax.dynamic_index_in_dim(send_group, position, 0, keepdims=False)
    outgoing = jnp.take(signature, own_row, axis=0)
    arrived = lax.all_to_all(outgoing, "grp", split_axis=0, concat_axis=0, tiled=True)
    pair_signal = jnp.take(arrived, pair_src, axis=0)
    live = jnp.arange(slots, dtype=jnp.int32) < live_count[0]
    bucket_index = pair_dst * TYPES + pair_type
    bucket_select_mask = (
        (jnp.arange(readers * TYPES, dtype=jnp.int32)[:, None] == bucket_index[None, :])
        & live[None, :]
    ).astype(jnp.bfloat16)
    times = jnp.arange(steps, dtype=jnp.int32)
    taps_index = jnp.arange(TAPS, dtype=jnp.int32)
    shifter = (times[None, None, :] - times[None, :, None] == taps_index[:, None, None]).astype(
        jnp.bfloat16
    )
    toeplitz = jnp.einsum(
        "cuk,ust->kcst", filters, shifter, preferred_element_type=jnp.float32
    ).astype(jnp.bfloat16)
    block = math.gcd(width, 64)

    def translate(index, partial_value):
        start = index * block
        signal_tile_block = lax.dynamic_slice_in_dim(pair_signal, start, block, 1)
        gathered = jnp.einsum(
            "ay,ydi->adi", bucket_select_mask, signal_tile_block, preferred_element_type=jnp.float32
        )
        gathered = gathered.reshape(readers, TYPES, block, steps)
        taps_block = lax.dynamic_slice_in_dim(toeplitz, start, block, 0).astype(jnp.float32)
        summed = jnp.einsum("dcks,kcst->dkt", gathered, taps_block, precision=lax.Precision.HIGHEST)
        return lax.dynamic_update_slice_in_dim(partial_value, summed, start, 1)

    partial_value = lax.fori_loop(
        0, width // block, translate, jnp.zeros((readers, width, steps), dtype=jnp.float32)
    )
    received = lax.all_to_all(partial_value, "grp", split_axis=0, concat_axis=0, tiled=True)
    self_received = lax.dynamic_index_in_dim(recv_group, position, 0, keepdims=False)
    owner_mask = (labels[:, None] == self_received[None, :]).astype(jnp.float32)
    incoming = jnp.einsum(
        "gr,rkt->gkt", owner_mask, received, precision=lax.Precision.HIGHEST
    ).astype(jnp.bfloat16)
    spread_field = jnp.einsum(
        "bk,gkt->bgt", projection, incoming, preferred_element_type=jnp.float32
    )
    field_terms = jnp.sum(spread_field * member.astype(jnp.float32)[:, :, None], axis=1)
    return lax.psum(field_terms, "dir").astype(jnp.bfloat16)


def solution(mesh):
    return jax.shard_map(
        local,
        mesh=mesh,
        in_specs=(
            P("grp", None),
            P("grp"),
            P("grp", "dir"),
            P(None, None, "dir"),
            P("grp"),
            P("grp"),
            P("grp"),
            P("grp"),
            P(),
            P(),
        ),
        out_specs=P("grp", None),
        check_vma=False,
    )
```

profile of v0, /device:TPU:0, one launch (start us, length us, event | category | flops | bytes accessed | tf_op | source)
XLA Modules:
  0.0 149.5 jit_solution(8783556434928073926)
XLA Ops:
  0.0 0.0 copy-start
  0.0 0.7 fusion.34
  0.7 0.7 compare_and_fusion
  1.4 0.7 fusion.36
  2.1 0.9 copy.17
  3.1 1.1 fusion.22
  4.2 0.1 copy.18
  4.3 0.6 gather_fusion
  4.9 0.9 broadcast_select_fusion.1
  5.9 7.3 %all-to-all-start = ((bf16[8,256,128]{2,1,0:T(8,128)(2,1)}), bf16[8,256,128]{2,1,0:T(8,128)(2,1)S(1)}, u32[]{:S(2)}, u32[]{:S(2)}) async-start(bf16[8,256,128]{2,1,0:T(8,128)(2,1)} %broadcast_select_fusion.1), calls=%async_computation | async-start | bytes 1048576 | tf_op jit(solution)/shard_map/all_to_all | solution.py:38
  13.2 0.0 copy-done
  13.2 14.5 %convert_bitcast_fusion = bf16[256,4,128,128]{0,3,1,2:T(8,128)(2,1)} fusion(s32[128,128]{1,0:T(8,128)S(1)} %iota_subtract_fusion, bf16[4,64,256]{2,1,0:T(8,128)(2,1)S(1)} %copy-done), kind=kOutput, calls=%fused_computation.18 | convolution fusion | flops 2165309440 | bytes 33751040 | tf_op jit(solution)/shard_map/cuk,ust->kcst/dot_general | solution.py:51
  27.7 0.0 copy-start.3
  27.7 0.0 copy-start.4
  27.7 0.0 copy-start.5
  27.7 46.1 %copy.19 = bf16[256,4,128,128]{3,2,1,0:T(8,128)(2,1)} copy(bf16[256,4,128,128]{0,3,1,2:T(8,128)(2,1)} %convert_bitcast_fusion) | data formatting | bytes 67108864
  74.4 0.0 copy-done.3
  74.5 0.0 copy-done.4
  74.5 0.0 copy-done.5
  74.5 0.0 all-to-all-done
  74.5 0.0 copy-start.1
  74.5 0.7 gather_fusion.1
  75.3 0.0 copy-start.2
  75.3 0.2 broadcast_select_fusion
  75.5 1.1 broadcast_in_dim.24.clone
  76.6 27.8 %while.14 = (s32[]{:T(128)}, f32[8,256,128]{2,1,0:T(8,128)}, bf16[256,4,128,128]{3,2,1,0:T(8,128)(2,1)}, bf16[16,256,128]{2,1,0:T(8,128)(2,1)S(1)}, s32[16]{0:T(...) while((s32[]{:T(128)}, f32[8,256,128]{2,1,0:T(8,128)}, ...), condition=%wide.region_1.2_spmd.clone, body=%wide.region_0.1_spmd.clone.sunk | while | flops 411043328 | bytes 12058871 | solution.py:67
  76.6 0.4 fusion.47
  77.0 5.7 %fusion.48 = f32[8,64,128]{2,0,1:T(8,128)S(1)} fusion(bf16[256,4,128,128]{3,2,1,0:T(8,128)(2,1)} %get-tuple-element.201, s32[]{:T(128)S(6)} %select_n.62, f32[8,4,64,128]{3,1,0,2:T(4,128)S(1)} %bitcast.53), kind=kOutput, calls=%fused_computation.5.clone.1 | convolution fusion | flops 402653184 | bytes 9699332 | tf_op jit(solution)/shard_map/while/body/eval_jaxpr/dcks,kcst->dkt/dot_general | solution.py:64
  82.7 0.8 copy_dynamic-update-slice_fusion.2
  83.5 0.4 fusion.47
  84.0 5.7 %fusion.48 = f32[8,64,128]{2,0,1:T(8,128)S(1)} fusion(bf16[256,4,128,128]{3,2,1,0:T(8,128)(2,1)} %get-tuple-element.201, s32[]{:T(128)S(6)} %select_n.62, f32[8,4,64,128]{3,1,0,2:T(4,128)S(1)} %bitcast.53), kind=kOutput, calls=%fused_computation.5.clone.1 | convolution fusion | flops 402653184 | bytes 9699332 | tf_op jit(solution)/shard_map/while/body/eval_jaxpr/dcks,kcst->dkt/dot_general | solution.py:64
  89.7 0.8 copy_dynamic-update-slice_fusion.2
  90.5 0.4 fusion.47
  90.9 5.7 %fusion.48 = f32[8,64,128]{2,0,1:T(8,128)S(1)} fusion(bf16[256,4,128,128]{3,2,1,0:T(8,128)(2,1)} %get-tuple-element.201, s32[]{:T(128)S(6)} %select_n.62, f32[8,4,64,128]{3,1,0,2:T(4,128)S(1)} %bitcast.53), kind=kOutput, calls=%fused_computation.5.clone.1 | convolution fusion | flops 402653184 | bytes 9699332 | tf_op jit(solution)/shard_map/while/body/eval_jaxpr/dcks,kcst->dkt/dot_general | solution.py:64
  96.6 0.8 copy_dynamic-update-slice_fusion.2
  97.4 0.4 fusion.47
  97.9 5.7 %fusion.48 = f32[8,64,128]{2,0,1:T(8,128)S(1)} fusion(bf16[256,4,128,128]{3,2,1,0:T(8,128)(2,1)} %get-tuple-element.201, s32[]{:T(128)S(6)} %select_n.62, f32[8,4,64,128]{3,1,0,2:T(4,128)S(1)} %bitcast.53), kind=kOutput, calls=%fused_computation.5.clone.1 | convolution fusion | flops 402653184 | bytes 9699332 | tf_op jit(solution)/shard_map/while/body/eval_jaxpr/dcks,kcst->dkt/dot_general | solution.py:64
  103.6 0.8 copy_dynamic-update-slice_fusion.2
  104.4 6.0 %all-to-all-start.1 = ((f32[8,256,128]{2,1,0:T(8,128)}), f32[8,256,128]{2,1,0:T(8,128)S(1)}, u32[]{:S(2)}, u32[]{:S(2)}) async-start(f32[8,256,128]{2,1,0:T(8,128)} %get-tuple-element.99), calls=%async_computation.1 | async-start | bytes 2097152 | tf_op jit(solution)/shard_map/all_to_all | solution.py:70
  110.4 0.7 dynamic-slice_bitcast_fusion
  111.0 24.7 %all-to-all-done.1 = f32[8,256,128]{2,1,0:T(8,128)S(1)} async-done(((f32[8,256,128]{2,1,0:T(8,128)}), f32[8,256,128]{2,1,0:T(8,128)S(1)}, u32[]{:S(2)}, u32[]{:S(2)}) %all-to-all-start.1) | async-done | bytes 1048608 | tf_op jit(solution)/shard_map/all_to_all | solution.py:70
  135.8 1.2 convolution_convert_fusion.1
  137.0 0.0 copy-done.2
  137.0 0.2 fusion.21
  137.2 11.5 %all-reduce.1 = bf16[256,128]{0,1:T(8,128)(2,1)S(1)} all-reduce(f32[256,128]{0,1:T(8,128)S(1)} %fusion.21), channel_id=1, replica_groups=mesh['grp'=8,'dir'=4] {'dir'}, use_global_device_ids=true, to_apply=%region_3.4 | all-reduce | flops 32768 | bytes 196608 | tf_op jit(solution)/shard_map/psum | solution.py:80
  148.7 0.7 copy.24
  149.4 0.0 copy-done.1
  (11 shorter events, 0.1 us)
Async XLA Ops:
  0.0 13.2 %copy-start = (bf16[4,64,256]{2,1,0:T(8,128)(2,1)S(1)}, bf16[4,64,256]{2,1,0:T(8,128)(2,1)}, u32[]{:S(2)}) copy-start(bf16[4,64,256]{2,1,0:T(8,128)(2,1)} %param.15) | copy-start | bytes 393220
  5.9 68.7 %all-to-all-start = ((bf16[8,256,128]{2,1,0:T(8,128)(2,1)}), bf16[8,256,128]{2,1,0:T(8,128)(2,1)S(1)}, u32[]{:S(2)}, u32[]{:S(2)}) async-start(bf16[8,256,128]{2,1,0:T(8,128)(2,1)} %broadcast_select_fusion.1), calls=%async_computation | async-start | bytes 1048576 | tf_op jit(solution)/shard_map/all_to_all | solution.py:38
  27.7 46.8 %copy-start.3 = (s32[16]{0:T(128)S(1)}, s32[16]{0:T(128)}, u32[]{:S(2)}) copy-start(s32[16]{0:T(128)} %param.16) | copy-start | bytes 196
  27.7 46.8 %copy-start.4 = (s32[16]{0:T(128)S(1)}, s32[16]{0:T(128)}, u32[]{:S(2)}) copy-start(s32[16]{0:T(128)} %param.18) | copy-start | bytes 196
  27.7 46.8 %copy-start.5 = (s32[16]{0:T(128)S(1)}, s32[16]{0:T(128)}, u32[]{:S(2)}) copy-start(s32[16]{0:T(128)} %param.17) | copy-start | bytes 196
  74.5 74.9 %copy-start.1 = (bf16[4,64,256]{2,1,0:T(8,128)(2,1)S(1)}, bf16[4,64,256]{2,1,0:T(8,128)(2,1)}, u32[]{:S(2)}) copy-start(bf16[4,64,256]{2,1,0:T(8,128)(2,1)} %param.15) | copy-start | bytes 393220
  75.3 61.7 %copy-start.2 = (bf16[256,256]{1,0:T(8,128)(2,1)S(1)}, bf16[256,256]{1,0:T(8,128)(2,1)}, u32[]{:S(2)}) copy-start(bf16[256,256]{1,0:T(8,128)(2,1)} %param.14) | copy-start | bytes 393220
  104.4 31.4 %all-to-all-start.1 = ((f32[8,256,128]{2,1,0:T(8,128)}), f32[8,256,128]{2,1,0:T(8,128)S(1)}, u32[]{:S(2)}, u32[]{:S(2)}) async-start(f32[8,256,128]{2,1,0:T(8,128)} %get-tuple-element.99), calls=%async_computation.1 | async-start | bytes 2097152 | tf_op jit(solution)/shard_map/all_to_all | solution.py:70
where the time goes:
time: 151 us; the launch traced here: 149 us
  local copies, waits for them, and re-layouts  54.3 us (36%)
  matrix products  41.5 us (27%)
  waiting for transfers between devices  24.7 us (16%)
  starting transfers between devices  13.3 us (9%)
  blocking collectives  11.5 us (8%)
  other arithmetic  3.23 us (2%)
    unnamed x14, local copies, waits for them, and re-layouts  47 us
    all_to_all x1, waiting for transfers between devices, local(): lax.all_to_all(partial_value, 'grp', split_axis=0, concat_axis=0, tiled=T...  24.7 us
    dot_general x4, matrix products, translate(): jnp.einsum('dcks,kcst->dkt', gathered, taps_block, precision=lax.Precisio...  22.9 us
    dot_general x1, matrix products, local(): jnp.einsum('cuk,ust->kcst', filters, shifter, preferred_element_type=jnp....  14.5 us
    psum x1, blocking collectives, local(): return lax.psum(field_terms, 'dir').astype(jnp.bfloat16)  11.5 us
    all_to_all x1, starting transfers between devices, local(): lax.all_to_all(outgoing, 'grp', split_axis=0, concat_axis=0, tiled=True)  7.31 us
    all_to_all x1, starting transfers between devices, local(): lax.all_to_all(partial_value, 'grp', split_axis=0, concat_axis=0, tiled=T...  6 us
    dynamic_update_slice x4, local copies, waits for them, and re-layouts, translate(): return lax.dynamic_update_slice_in_dim(partial_value, summed, start, 1)  3.13 us
  transfers between devices with their start and end apart: 2, of which 1 were waited for; matrix products, arithmetic and copies ran while one was open for 41% of the time, Pallas kernels for 0%

commit v1 on v0

v1 whole, which is shorter than its diff:
```python
import functools

import jax
import jax.numpy as jnp
import numpy as np
from jax import lax
from jax.experimental import pallas as pl
from jax.experimental.pallas import tpu as pltpu
from jax.sharding import PartitionSpec as P

G_DEV = 2
LANES = 128
TABLE_ROWS = 16
BF16 = jnp.bfloat16
F32 = jnp.float32

VMEM = pl.BlockSpec(memory_space=pltpu.VMEM)
SMEM = pl.BlockSpec(memory_space=pltpu.SMEM)


def halves(table):
    high = table.astype(jnp.bfloat16)
    low = (table - high.astype(np.float64)).astype(jnp.bfloat16)
    return high, low


def wave_tables(steps):
    angle = np.pi * np.outer(np.arange(steps), np.arange(steps) + 0.5) / steps
    forward = np.concatenate([np.cos(angle), -np.sin(angle)], axis=1)
    inverse = forward.T / steps
    return halves(forward), halves(inverse)


def dot(a, b, dims=((1,), (0,))):
    return lax.dot_general(a, b, (dims, ((), ())), preferred_element_type=F32)


def member_column(group_row):
    rows = group_row.shape[1]
    return jnp.broadcast_to(group_row.astype(F32), (LANES, rows)).T[:, :1]


def project_kernel(
    readers,
    slots,
    position_ref,
    currents_ref,
    group_ref,
    projection_ref,
    src_ref,
    dst_ref,
    type_ref,
    live_ref,
    send_ref,
    recv_ref,
    out_ref,
):
    steps = currents_ref.shape[1]
    block = projection_ref.shape[1] // readers
    rows = out_ref.shape[1]
    me = position_ref[0]
    column = member_column(group_ref[...])
    series = currents_ref[...].astype(F32)
    spread = jnp.concatenate(
        [jnp.where(column == g, series, 0.0).astype(BF16) for g in range(G_DEV)], axis=1
    )
    signature = dot(projection_ref[...], spread, ((0,), (0,))).astype(BF16)
    for owner in range(readers):
        for g in range(G_DEV):
            out_ref[owner, pl.ds(g * block, block), :] = signature[
                owner * block : (owner + 1) * block, g * steps : (g + 1) * steps
            ]

    pack = max(1, LANES // slots)
    first = lax.rem(me, pack) * slots
    lane = lax.broadcasted_iota(jnp.int32, (TABLE_ROWS, LANES), 1)
    row = lax.broadcasted_iota(jnp.int32, (TABLE_ROWS, LANES), 0)
    live = live_ref[0]

    def add_slot(p, table):
        src = src_ref[p]
        dst = dst_ref[p]
        source = src * G_DEV + send_ref[src, me]
        target = dst * G_DEV + recv_ref[dst, me] + 1
        target = jnp.where(p < live, target, 0)
        value = jnp.where(row == 0, source, jnp.where(row == 1, target, type_ref[p]))
        return jnp.where(lane == first + p, value, table)

    table = lax.fori_loop(
        0, slots, add_slot, jnp.zeros((TABLE_ROWS, LANES), jnp.int32), unroll=slots <= 16
    )
    table = table.astype(F32).astype(BF16)
    for owner in range(readers):
        out_ref[owner, pl.ds(rows - TABLE_ROWS, TABLE_ROWS), :] = table


def filter_kernel(filters_ref, wave_ref, out_ref):
    types, taps, width = filters_ref.shape
    wave = wave_ref[...]
    for c in range(types):
        taps_c = filters_ref[c]
        out_ref[c] = dot(jnp.concatenate([taps_c, taps_c], axis=0), wave, ((0,), (0,)))


def split(value):
    high = value.astype(BF16)
    return high, (value - high.astype(F32)).astype(BF16)


def translate_kernel(
    readers,
    slots,
    block,
    position_ref,
    arrived_ref,
    response_ref,
    forward_ref,
    inverse_high_ref,
    inverse_low_ref,
    out_ref,
    order_ref,
    wave_ref,
    product_ref,
    result_ref,
):
    types = response_ref.shape[0]
    steps = inverse_high_ref.shape[1]
    groups = readers * G_DEV
    rows = G_DEV * block + TABLE_ROWS
    base = position_ref[0] * block

    for owner in range(readers):
        part = arrived_ref[pl.ds(owner * rows, G_DEV * block), :]
        order_ref[pl.ds(owner * G_DEV * block, G_DEV * block), :] = part.astype(F32)

    pack = max(1, LANES // slots)
    count = jnp.zeros((types * groups, groups), F32)
    bucket_row = lax.broadcasted_iota(jnp.int32, (types * groups, LANES), 0)
    group_row = lax.broadcasted_iota(jnp.int32, (groups, LANES), 0)
    for first in range(0, readers, pack):
        table = jnp.zeros((TABLE_ROWS, LANES), F32)
        for owner in range(first, min(first + pack, readers)):
            start = owner * rows + G_DEV * block
            table = table + arrived_ref[pl.ds(start, TABLE_ROWS), :].astype(F32)
        table = table.astype(jnp.int32)
        source, target, kind = table[0:1], table[1:2], table[2:3]
        bucket = jnp.where(target > 0, kind * groups + target - 1, -1)
        to_bucket = (bucket_row == bucket).astype(F32).astype(BF16)
        from_group = (group_row == source).astype(F32).astype(BF16)
        count = count + dot(to_bucket, from_group, ((1,), (1,)))
    count_high, count_low = split(count)
    if readers * slots > 256:
        count_parts = jnp.concatenate([count_high, count_high, count_low, count_low], axis=1)
    else:
        count_parts = jnp.concatenate([count_high, count_high], axis=1)

    forward = forward_ref[...]
    for k in range(block):
        signal = order_ref[pl.ds(k, groups, stride=block), :].astype(BF16)
        wave_ref[pl.ds(k * groups, groups), :] = signal
    signals = wave_ref[...]
    waves = dot(jnp.concatenate([signals, signals], axis=1), forward)
    for k in range(block):
        high, low = split(waves[k * groups : (k + 1) * groups])
        if readers * slots > 256:
            parts = jnp.concatenate([high, low, high, low], axis=0)
        else:
            parts = jnp.concatenate([high, low], axis=0)
        gathered = dot(count_parts, parts)
        real = jnp.zeros((groups, steps), F32)
        imag = jnp.zeros((groups, steps), F32)
        for c in range(types):
            response = response_ref[c, pl.ds(base + k, 1), :]
            response_real, response_imag = response[:, :steps], response[:, steps:]
            bucket = gathered[c * groups : (c + 1) * groups]
            bucket_real, bucket_imag = bucket[:, :steps], bucket[:, steps:]
            real = real + (bucket_real * response_real - bucket_imag * response_imag)
            imag = imag + (bucket_real * response_imag + bucket_imag * response_real)
        product_ref[pl.ds(k * groups, groups), pl.ds(0, steps)] = real
        product_ref[pl.ds(k * groups, groups), pl.ds(steps, steps)] = imag
    high, low = split(product_ref[...])
    inverse_high = inverse_high_ref[...]
    result_ref[...] = (
        dot(high, inverse_high) + dot(low, inverse_high) + dot(high, inverse_low_ref[...])
    )
    for g in range(groups):
        out_ref[pl.ds(g * block, block), :] = result_ref[
            pl.ds(g, block, stride=groups), :
        ].astype(BF16)


def field_kernel(readers, block, group_ref, projection_ref, incoming_ref, out_ref):
    column = member_column(group_ref[...])
    projection = projection_ref[...]
    field = None
    for g in range(G_DEV):
        incoming = jnp.concatenate(
            [
                incoming_ref[pl.ds((part * G_DEV + g) * block, block), :]
                for part in range(readers)
            ],
            axis=0,
        )
        term = dot(projection, incoming)
        field = term if g == 0 else jnp.where(column == g, term, field)
    out_ref[...] = field.astype(BF16)


def local(
    currents,
    basis_group,
    projection,
    filters,
    pair_src,
    pair_dst,
    pair_type,
    live_count,
    send_group,
    recv_group,
):
    readers = lax.axis_size("grp")
    spans = lax.axis_size("dir")
    steps = currents.shape[1]
    basis, width = projection.shape
    types, taps, _ = filters.shape
    slots = pair_src.shape[0]
    block = width // readers
    groups = readers * G_DEV
    rows = G_DEV * block + TABLE_ROWS
    position = lax.axis_index("grp").astype(jnp.int32).reshape(1)
    (forward_high, forward_low), (inverse_high, inverse_low) = wave_tables(steps)
    group_row = basis_group.reshape(1, basis)

    outgoing = pl.pallas_call(
        functools.partial(project_kernel, readers, slots),
        out_shape=jax.ShapeDtypeStruct((readers, rows, steps), BF16),
        in_specs=[SMEM, VMEM, VMEM, VMEM, SMEM, SMEM, SMEM, SMEM, SMEM, SMEM],
        out_specs=VMEM,
    )(
        position,
        currents,
        group_row,
        projection,
        pair_src,
        pair_dst,
        pair_type,
        live_count,
        send_group,
        recv_group,
    )
    arrived = lax.all_to_all(outgoing, "grp", split_axis=0, concat_axis=0, tiled=True)
    response = pl.pallas_call(
        filter_kernel,
        out_shape=jax.ShapeDtypeStruct((types, width, 2 * steps), F32),
        in_specs=[VMEM, VMEM],
        out_specs=VMEM,
        cost_estimate=pl.CostEstimate(
            flops=8 * types * width * taps * steps, bytes_accessed=2**21, transcendentals=0
        ),
    )(filters, np.concatenate([forward_high[:taps], forward_low[:taps]], axis=0))
    incoming = pl.pallas_call(
        functools.partial(translate_kernel, readers, slots, block),
        out_shape=jax.ShapeDtypeStruct((groups * block, steps), BF16),
        in_specs=[SMEM, VMEM, VMEM, VMEM, VMEM, VMEM],
        out_specs=VMEM,
        scratch_shapes=[
            pltpu.VMEM((groups * block, steps), F32),
            pltpu.VMEM((groups * block, steps), BF16),
            pltpu.VMEM((groups * block, 2 * steps), F32),
            pltpu.VMEM((groups * block, steps), F32),
        ],
    )(
        position,
        arrived.reshape(readers * rows, steps),
        response,
        np.concatenate([forward_high, forward_low], axis=0),
        inverse_high,
        inverse_low,
    )
    incoming = incoming.reshape(readers, G_DEV * block, steps)
    own = lax.all_to_all(incoming, "grp", split_axis=0, concat_axis=0, tiled=True)
    term = pl.pallas_call(
        functools.partial(field_kernel, readers, block),
        out_shape=jax.ShapeDtypeStruct((basis, steps), BF16),
        in_specs=[VMEM, VMEM, VMEM],
        out_specs=VMEM,
    )(group_row, projection, own.reshape(groups * block, steps))

    sums = [term.astype(F32)]
    for other in range(1, spans):
        pairs = [(d, d ^ other) for d in range(spans)]
        sums.append(lax.ppermute(term, "dir", pairs).astype(F32))
    while len(sums) > 1:
        sums = [sums[i] + sums[i + 1] for i in range(0, len(sums), 2)]
    return sums[0].astype(BF16)


def solution(mesh):
    return jax.shard_map(
        local,
        mesh=mesh,
        in_specs=(
            P("grp", None),
            P("grp"),
            P("grp", "dir"),
            P(None, None, "dir"),
            P("grp"),
            P("grp"),
            P("grp"),
            P("grp"),
            P(),
            P(),
        ),
        out_specs=P("grp", None),
        check_vma=False,
    )
```

time: 151 us -> 42.4 us (0.28)
  local copies, waits for them, and re-layouts: 54.3 us -> 0.66 us
  matrix products: 41.5 us -> 0 us
  waiting for transfers between devices: 24.7 us -> 9.51 us
  Pallas kernels: 0 us -> 9.13 us
  starting transfers between devices: 13.3 us -> 9.17 us
  other arithmetic: 3.23 us -> 1.51 us
    unnamed x14 -> x2, local copies, waits for them, and re-layouts: 47 us -> 0.66 us
    dot_general x12 -> x0, matrix products: 41.5 us -> none  [the longest x4 22.9 us: translate(): jnp.einsum('dcks,kcst->dkt', gathered, taps_block, precision=lax.Precisio...]
    all_to_all x1 -> x0, waiting for transfers between devices: 24.7 us -> none  [local(): lax.all_to_all(partial_value, 'grp', split_axis=0, concat_axis=0, tiled=T...]
    psum x1 -> x0, blocking collectives: 11.5 us -> none  [local(): return lax.psum(field_terms, 'dir').astype(jnp.bfloat16)]
    all_to_all x0 -> x1, blocking collectives: none -> 11.3 us  [local(): lax.all_to_all(incoming, 'grp', split_axis=0, concat_axis=0, tiled=True)]
    pallas_call x0 -> x4, Pallas kernels: none -> 9.13 us  [the longest x1 3.08 us: local(): pl.pallas_call(functools.partial(translate_kernel, readers, slots, block)...]
    all_to_all x1 -> x0, starting transfers between devices: 6 us -> none  [local(): lax.all_to_all(partial_value, 'grp', split_axis=0, concat_axis=0, tiled=T...]
    all_to_all x1, waiting for transfers between devices: 0.01 us -> 5.36 us  [local(): lax.all_to_all(outgoing, 'grp', split_axis=0, concat_axis=0, tiled=True)]
  transfers between devices with their start and end apart: 2 -> 4, of which waited for: 1 -> 3; matrix products, arithmetic and copies ran while one was open for 41% -> 0% of each run, Pallas kernels for 0% -> 5%
where the time goes in v1:
time: 42.4 us; the launch traced here: 42 us
  blocking collectives  11.3 us (27%)
  waiting for transfers between devices  9.51 us (22%)
  starting transfers between devices  9.17 us (22%)
  Pallas kernels  9.13 us (22%)
  other arithmetic  1.51 us (4%)
  local copies, waits for them, and re-layouts  0.66 us (2%)
  between operations  0.66 us (2%)
    all_to_all x1, blocking collectives, local(): lax.all_to_all(incoming, 'grp', split_axis=0, concat_axis=0, tiled=True)  11.3 us
    all_to_all x1, starting transfers between devices, local(): lax.all_to_all(outgoing, 'grp', split_axis=0, concat_axis=0, tiled=True)  7.31 us
    all_to_all x1, waiting for transfers between devices, local(): lax.all_to_all(outgoing, 'grp', split_axis=0, concat_axis=0, tiled=True)  5.36 us
    ppermute x3, waiting for transfers between devices, local(): sums.append(lax.ppermute(term, 'dir', pairs).astype(F32))  4.15 us
    pallas_call x1, Pallas kernels, local(): pl.pallas_call(functools.partial(translate_kernel, readers, slots, block)...  3.08 us
    pallas_call x1, Pallas kernels, local(): pl.pallas_call(filter_kernel, out_shape=jax.ShapeDtypeStruct((types, widt...  2.2 us
    pallas_call x1, Pallas kernels, local(): pl.pallas_call(functools.partial(project_kernel, readers, slots), out_sha...  2.02 us
    ppermute x3, starting transfers between devices, local(): sums.append(lax.ppermute(term, 'dir', pairs).astype(F32))  1.86 us
  transfers between devices with their start and end apart: 4, of which 3 were waited for; matrix products, arithmetic and copies ran while one was open for 0% of the time, Pallas kernels for 5%

profile of v1, /device:TPU:0, one launch (start us, length us, event | category | flops | bytes accessed | tf_op | source)
XLA Modules:
  0.0 42.0 jit_solution(4804303661318952429)
XLA Ops:
  0.7 2.0 %shard_map.136 = bf16[8,80,128]{2,1,0:T(8,128)(2,1)} custom-call(s32[1]{0:T(128)} %bitcast.1.position_ref, bf16[256,128]{1,0:T(8,128)(2,1)} %currents_ref.1, s32[1,256]{1,0:T(1,128)} %bitcast.8, bf16[256,256]{1,0:T(8,128)(2,1)} %projection_ref.3, s32[16]{0:T(128)} %src_ref.1, s32[16]{0:T(128)} %dst_ref.1, s32[16]{0:T(128)} %type_ref.1, s32[1]{0:T(128)S(6)} %copy.15.live_ref, ...), custom_call_target="tpu_custom_call" | custom-call | tf_op jit(solution)/shard_map/pallas_call | solution.py:234
  2.7 7.3 %all-to-all-start = ((bf16[8,80,128]{2,1,0:T(8,128)(2,1)}), bf16[8,80,128]{2,1,0:T(8,128)(2,1)S(1)}, u32[]{:S(2)}, u32[]{:S(2)}) async-start(bf16[8,80,128]{2,1,0:T(8,128)(2,1)} %shard_map.136), calls=%async_computation | async-start | bytes 327680 | tf_op jit(solution)/shard_map/all_to_all | solution.py:251
  10.0 2.2 %shard_map.137.response_ref = f32[4,256,256]{2,1,0:T(8,128)} custom-call(bf16[4,64,256]{2,1,0:T(8,128)(2,1)} %filters_ref.1, bf16[128,256]{1,0:T(8,128)(2,1)} %constant.14.clone.wave_ref), custom_call_target="tpu_custom_call" | custom-call | flops 67108864 | bytes 2097152 | tf_op jit(solution)/shard_map/pallas_call | solution.py:252
  12.2 5.4 %all-to-all-done = bf16[8,80,128]{2,1,0:T(8,128)(2,1)S(1)} async-done(((bf16[8,80,128]{2,1,0:T(8,128)(2,1)}), bf16[8,80,128]{2,1,0:T(8,128)(2,1)S(1)}, u32[]{:S(2)}, u32[]{:S(2)}) %all-to-all-start) | async-done | bytes 163872 | tf_op jit(solution)/shard_map/all_to_all | solution.py:251
  17.6 0.0 copy-start
  17.6 0.7 %copy-done = bf16[8,80,128]{2,1,0:T(8,128)(2,1)} copy-done((bf16[8,80,128]{2,1,0:T(8,128)(2,1)}, bf16[8,80,128]{2,1,0:T(8,128)(2,1)S(1)}, u32[]{:S(2)}) %copy-start) | copy-done | bytes 163864
  18.2 3.1 %shard_map.138 = bf16[512,128]{1,0:T(8,128)(2,1)} custom-call(s32[1]{0:T(128)} %bitcast.1.position_ref, bf16[640,128]{1,0:T(8,128)(2,1)} %bitcast.5, f32[4,256,256]{2,1,0:T(8,128)} %shard_map.137.response_ref, bf16[256,256]{1,0:T(8,128)(2,1)} %constant.15.clone.forward_ref, bf16[256,128]{1,0:T(8,128)(2,1)} %constant.16.clone.inverse_high_ref, ...), custom_call_target="tpu_custom_call" | custom-call | tf_op jit(solution)/shard_map/pallas_call | solution.py:261
  21.3 11.3 %all_to_all.10 = bf16[8,64,128]{2,1,0:T(8,128)(2,1)} all-to-all(bf16[8,64,128]{2,1,0:T(8,128)(2,1)} %bitcast.6), channel_id=1, replica_groups=mesh['grp'=8,'dir'=4] {'grp'}, dimensions={0} | all-to-all | bytes 262144 | tf_op jit(solution)/shard_map/all_to_all | solution.py:281
  32.6 1.8 %shard_map.139 = bf16[256,128]{1,0:T(8,128)(2,1)} custom-call(s32[1,256]{1,0:T(1,128)} %bitcast.9, bf16[256,256]{1,0:T(8,128)(2,1)} %projection_ref.3, bf16[512,128]{1,0:T(8,128)(2,1)} %bitcast.7), custom_call_target="tpu_custom_call" | custom-call | tf_op jit(solution)/shard_map/pallas_call | solution.py:282
  34.4 0.0 collective-permute-start.2
  34.5 1.5 %collective-permute-start.1 = (bf16[256,128]{1,0:T(8,128)(2,1)}, bf16[256,128]{1,0:T(8,128)(2,1)S(1)}, u32[]{:S(2)}, u32[]{:S(2)}) collective-permute-start(bf16[256,128]{1,0:T(8,128)(2,1)} %shard_map.139), channel_id=1, source_target_pairs={{0,2},{1,3},{2,0},{3,1},{4,6},{5,7},{6,4},{7,5},{8,10},{9,11},{10,... | collective-permute-start | bytes 196616 | tf_op jit(solution)/shard_map/ppermute | solution.py:292
  35.9 0.4 collective-permute-start
  36.3 2.7 %collective-permute-done.2 = bf16[256,128]{1,0:T(8,128)(2,1)S(1)} collective-permute-done((bf16[256,128]{1,0:T(8,128)(2,1)}, bf16[256,128]{1,0:T(8,128)(2,1)S(1)}, u32[]{:S(2)}, u32[]{:S(2)}) %collective-permute-start.2) | collective-permute-done | bytes 65568 | tf_op jit(solution)/shard_map/ppermute | solution.py:292
  39.0 1.4 %collective-permute-done.1 = bf16[256,128]{1,0:T(8,128)(2,1)S(1)} collective-permute-done((bf16[256,128]{1,0:T(8,128)(2,1)}, bf16[256,128]{1,0:T(8,128)(2,1)S(1)}, u32[]{:S(2)}, u32[]{:S(2)}) %collective-permute-start.1) | collective-permute-done | bytes 65568 | tf_op jit(solution)/shard_map/ppermute | solution.py:292
  40.5 0.0 collective-permute-done
  40.5 1.5 %add_convert_fusion = bf16[256,128]{1,0:T(8,128)(2,1)} fusion(bf16[256,128]{1,0:T(8,128)(2,1)S(1)} %collective-permute-done.2, bf16[256,128]{1,0:T(8,128)(2,1)S(1)} %collective-permute-done.1, bf16[256,128]{1,0:T(8,128)(2,1)S(1)} %collective-permute-done, bf16[256,128]{1,0:T(8,128)(2,1)} %shard_map.139), kind=kLoop, calls=%fused_computation | loop fusion | flops 262144 | bytes 327680 | tf_op jit(solution)/shard_map/convert_element_type | solution.py:295
Async XLA Ops:
  2.7 14.9 %all-to-all-start = ((bf16[8,80,128]{2,1,0:T(8,128)(2,1)}), bf16[8,80,128]{2,1,0:T(8,128)(2,1)S(1)}, u32[]{:S(2)}, u32[]{:S(2)}) async-start(bf16[8,80,128]{2,1,0:T(8,128)(2,1)} %shard_map.136), calls=%async_computation | async-start | bytes 327680 | tf_op jit(solution)/shard_map/all_to_all | solution.py:251
  17.6 0.7 %copy-start = (bf16[8,80,128]{2,1,0:T(8,128)(2,1)}, bf16[8,80,128]{2,1,0:T(8,128)(2,1)S(1)}, u32[]{:S(2)}) copy-start(bf16[8,80,128]{2,1,0:T(8,128)(2,1)S(1)} %all-to-all-done) | copy-start | bytes 491524
  34.4 4.6 %collective-permute-start.2 = (bf16[256,128]{1,0:T(8,128)(2,1)}, bf16[256,128]{1,0:T(8,128)(2,1)S(1)}, u32[]{:S(2)}, u32[]{:S(2)}) collective-permute-start(bf16[256,128]{1,0:T(8,128)(2,1)} %shard_map.139), channel_id=1, source_target_pairs={{0,3},{1,2},{2,1},{3,0},{4,7},{5,6},{6,5},{7,4},{8,11},{9,10},{10,... | collective-permute-start | bytes 196616 | tf_op jit(solution)/shard_map/ppermute | solution.py:292
  34.5 6.0 %collective-permute-start.1 = (bf16[256,128]{1,0:T(8,128)(2,1)}, bf16[256,128]{1,0:T(8,128)(2,1)S(1)}, u32[]{:S(2)}, u32[]{:S(2)}) collective-permute-start(bf16[256,128]{1,0:T(8,128)(2,1)} %shard_map.139), channel_id=1, source_target_pairs={{0,2},{1,3},{2,0},{3,1},{4,6},{5,7},{6,4},{7,5},{8,10},{9,11},{10,... | collective-permute-start | bytes 196616 | tf_op jit(solution)/shard_map/ppermute | solution.py:292
  35.9 4.5 %collective-permute-start = (bf16[256,128]{1,0:T(8,128)(2,1)}, bf16[256,128]{1,0:T(8,128)(2,1)S(1)}, u32[]{:S(2)}, u32[]{:S(2)}) collective-permute-start(bf16[256,128]{1,0:T(8,128)(2,1)} %shard_map.139), channel_id=1, source_target_pairs={{0,1},{1,0},{2,3},{3,2},{4,5},{5,4},{6,7},{7,6},{8,9},{9,8},{10,11... | collective-permute-start | bytes 196616 | tf_op jit(solution)/shard_map/ppermute | solution.py:292

commit v2 on v1

--- a/solution.py
+++ b/solution.py
@@ -10,12 +10,17 @@
 
 G_DEV = 2
 LANES = 128
-TABLE_ROWS = 16
+TABLE_ROWS = 8
 BF16 = jnp.bfloat16
 F32 = jnp.float32
 
 VMEM = pl.BlockSpec(memory_space=pltpu.VMEM)
-SMEM = pl.BlockSpec(memory_space=pltpu.SMEM)
+FAR = pl.BlockSpec(memory_space=pl.ANY)
+PARAMS = pltpu.CompilerParams(vmem_limit_bytes=16 * 2**20)
+
+
+def near(value):
+    return pltpu.with_memory_space_constraint(value, pltpu.VMEM)
 
 
 def halves(table):
@@ -35,15 +40,19 @@
     return lax.dot_general(a, b, (dims, ((), ())), preferred_element_type=F32)
 
 
-def member_column(group_row):
-    rows = group_row.shape[1]
-    return jnp.broadcast_to(group_row.astype(F32), (LANES, rows)).T[:, :1]
-
-
 def project_kernel(
     readers,
     slots,
-    position_ref,
+    currents_hbm,
+    group_hbm,
+    projection_hbm,
+    src_hbm,
+    dst_hbm,
+    type_hbm,
+    live_hbm,
+    send_hbm,
+    recv_hbm,
+    out_ref,
     currents_ref,
     group_ref,
     projection_ref,
@@ -53,29 +62,41 @@
     live_ref,
     send_ref,
     recv_ref,
-    out_ref,
+    sems,
 ):
+    wide = [
+        pltpu.make_async_copy(source, target, sems.at[i])
+        for i, (source, target) in enumerate(
+            [(projection_hbm, projection_ref), (currents_hbm, currents_ref), (group_hbm, group_ref)]
+        )
+    ]
+    small = [
+        pltpu.make_async_copy(source, target, sems.at[len(wide) + i])
+        for i, (source, target) in enumerate(
+            [
+                (src_hbm, src_ref),
+                (dst_hbm, dst_ref),
+                (type_hbm, type_ref),
+                (live_hbm, live_ref),
+                (send_hbm, send_ref),
+                (recv_hbm, recv_ref),
+            ]
+        )
+    ]
+    for copy in wide + small:
+        copy.start()
+
     steps = currents_ref.shape[1]
     block = projection_ref.shape[1] // readers
     rows = out_ref.shape[1]
-    me = position_ref[0]
-    column = member_column(group_ref[...])
-    series = currents_ref[...].astype(F32)
-    spread = jnp.concatenate(
-        [jnp.where(column == g, series, 0.0).astype(BF16) for g in range(G_DEV)], axis=1
-    )
-    signature = dot(projection_ref[...], spread, ((0,), (0,))).astype(BF16)
-    for owner in range(readers):
-        for g in range(G_DEV):
-            out_ref[owner, pl.ds(g * block, block), :] = signature[
-                owner * block : (owner + 1) * block, g * steps : (g + 1) * steps
-            ]
-
+    me = lax.axis_index("grp")
     pack = max(1, LANES // slots)
     first = lax.rem(me, pack) * slots
     lane = lax.broadcasted_iota(jnp.int32, (TABLE_ROWS, LANES), 1)
     row = lax.broadcasted_iota(jnp.int32, (TABLE_ROWS, LANES), 0)
-    live = live_ref[0]
+    for copy in small + wide:
+        copy.wait()
+    live = live_ref[0, 0]
 
     def add_slot(p, table):
         src = src_ref[p]
@@ -93,13 +114,26 @@
     for owner in range(readers):
         out_ref[owner, pl.ds(rows - TABLE_ROWS, TABLE_ROWS), :] = table
 
-
-def filter_kernel(filters_ref, wave_ref, out_ref):
+    pattern = projection_ref[...].T
+    series = currents_ref[...]
+    for g in range(G_DEV):
+        member = (group_ref[...] == g).astype(F32).astype(BF16)
+        signature = dot(pattern * member, series).astype(BF16)
+        for owner in range(readers):
+            out_ref[owner, pl.ds(g * block, block), :] = signature[
+                owner * block : (owner + 1) * block
+            ]
+
+
+def filter_kernel(group_ref, filters_ref, wave_ref, out_ref, column_ref):
     types, taps, width = filters_ref.shape
     wave = wave_ref[...]
     for c in range(types):
         taps_c = filters_ref[c]
         out_ref[c] = dot(jnp.concatenate([taps_c, taps_c], axis=0), wave, ((0,), (0,)))
+    column_ref[...] = jnp.broadcast_to(
+        group_ref[...].astype(F32), (LANES, group_ref.shape[1])
+    ).T
 
 
 def split(value):
@@ -111,7 +145,6 @@
     readers,
     slots,
     block,
-    position_ref,
     arrived_ref,
     response_ref,
     forward_ref,
@@ -127,7 +160,7 @@
     steps = inverse_high_ref.shape[1]
     groups = readers * G_DEV
     rows = G_DEV * block + TABLE_ROWS
-    base = position_ref[0] * block
+    base = lax.axis_index("grp") * block
 
     for owner in range(readers):
         part = arrived_ref[pl.ds(owner * rows, G_DEV * block), :]
@@ -189,8 +222,8 @@
         ].astype(BF16)
 
 
-def field_kernel(readers, block, group_ref, projection_ref, incoming_ref, out_ref):
-    column = member_column(group_ref[...])
+def field_kernel(readers, block, column_ref, projection_ref, incoming_ref, out_ref):
+    column = column_ref[:, :1]
     projection = projection_ref[...]
     field = None
     for g in range(G_DEV):
@@ -227,42 +260,49 @@
     block = width // readers
     groups = readers * G_DEV
     rows = G_DEV * block + TABLE_ROWS
-    position = lax.axis_index("grp").astype(jnp.int32).reshape(1)
     (forward_high, forward_low), (inverse_high, inverse_low) = wave_tables(steps)
     group_row = basis_group.reshape(1, basis)
 
-    outgoing = pl.pallas_call(
-        functools.partial(project_kernel, readers, slots),
-        out_shape=jax.ShapeDtypeStruct((readers, rows, steps), BF16),
-        in_specs=[SMEM, VMEM, VMEM, VMEM, SMEM, SMEM, SMEM, SMEM, SMEM, SMEM],
-        out_specs=VMEM,
-    )(
-        position,
+    inputs = (
         currents,
         group_row,
         projection,
         pair_src,
         pair_dst,
         pair_type,
-        live_count,
+        live_count.reshape(1, 1),
         send_group,
         recv_group,
     )
+    outgoing = pl.pallas_call(
+        functools.partial(project_kernel, readers, slots),
+        out_shape=jax.ShapeDtypeStruct((readers, rows, steps), BF16),
+        in_specs=[FAR] * len(inputs),
+        out_specs=VMEM,
+        scratch_shapes=[pltpu.VMEM(x.shape, x.dtype) for x in inputs[:3]]
+        + [pltpu.SMEM(x.shape, x.dtype) for x in inputs[3:]]
+        + [pltpu.SemaphoreType.DMA((len(inputs),))],
+    )(*inputs)
     arrived = lax.all_to_all(outgoing, "grp", split_axis=0, concat_axis=0, tiled=True)
-    response = pl.pallas_call(
+    response, column = pl.pallas_call(
         filter_kernel,
-        out_shape=jax.ShapeDtypeStruct((types, width, 2 * steps), F32),
-        in_specs=[VMEM, VMEM],
-        out_specs=VMEM,
+        out_shape=(
+            pltpu.VMEM((types, width, 2 * steps), F32),
+            pltpu.VMEM((basis, LANES), F32),
+        ),
+        in_specs=[VMEM, VMEM, VMEM],
+        out_specs=(VMEM, VMEM),
+        compiler_params=PARAMS,
         cost_estimate=pl.CostEstimate(
             flops=8 * types * width * taps * steps, bytes_accessed=2**21, transcendentals=0
         ),
-    )(filters, np.concatenate([forward_high[:taps], forward_low[:taps]], axis=0))
+    )(group_row, filters, np.concatenate([forward_high[:taps], forward_low[:taps]], axis=0))
     incoming = pl.pallas_call(
         functools.partial(translate_kernel, readers, slots, block),
-        out_shape=jax.ShapeDtypeStruct((groups * block, steps), BF16),
-        in_specs=[SMEM, VMEM, VMEM, VMEM, VMEM, VMEM],
+        out_shape=pltpu.VMEM((groups * block, steps), BF16),
+        in_specs=[VMEM, VMEM, VMEM, VMEM, VMEM],
         out_specs=VMEM,
+        compiler_params=PARAMS,
         scratch_shapes=[
             pltpu.VMEM((groups * block, steps), F32),
             pltpu.VMEM((groups * block, steps), BF16),
@@ -270,21 +310,21 @@
             pltpu.VMEM((groups * block, steps), F32),
         ],
     )(
-        position,
-        arrived.reshape(readers * rows, steps),
-        response,
-        np.concatenate([forward_high, forward_low], axis=0),
-        inverse_high,
-        inverse_low,
+        near(arrived.reshape(readers * rows, steps)),
+        near(response),
+        near(jnp.asarray(np.concatenate([forward_high, forward_low], axis=0))),
+        near(jnp.asarray(inverse_high)),
+        near(jnp.asarray(inverse_low)),
     )
     incoming = incoming.reshape(readers, G_DEV * block, steps)
     own = lax.all_to_all(incoming, "grp", split_axis=0, concat_axis=0, tiled=True)
     term = pl.pallas_call(
         functools.partial(field_kernel, readers, block),
-        out_shape=jax.ShapeDtypeStruct((basis, steps), BF16),
+        out_shape=pltpu.VMEM((basis, steps), BF16),
         in_specs=[VMEM, VMEM, VMEM],
         out_specs=VMEM,
-    )(group_row, projection, own.reshape(groups * block, steps))
+        compiler_params=PARAMS,
+    )(near(column), near(projection), near(own.reshape(groups * block, steps)))
 
     sums = [term.astype(F32)]
     for other in range(1, spans):

time: 42.4 us -> 35.7 us (0.84)
  Pallas kernels: 9.13 us -> 3.64 us
  waiting for transfers between devices: 9.51 us -> 11 us
  blocking collectives: 11.3 us -> 9.87 us
  other arithmetic: 1.51 us -> 0.67 us
  local copies, waits for them, and re-layouts: 0.66 us -> 0.05 us
    pallas_call x1, Pallas kernels: 3.08 us -> 1.14 us  [local(): pl.pallas_call(functools.partial(translate_kernel, readers, slots, block)...]
    pallas_call x1, Pallas kernels: 2.2 us -> 0.32 us  [local(): pl.pallas_call(filter_kernel, out_shape=(pltpu.VMEM((types, width, 2 * st...]
    all_to_all x1, waiting for transfers between devices: 5.36 us -> 7.07 us  [local(): lax.all_to_all(outgoing, 'grp', split_axis=0, concat_axis=0, tiled=True)]
    pallas_call x1, Pallas kernels: 1.83 us -> 0.21 us  [local(): pl.pallas_call(functools.partial(field_kernel, readers, block), out_shape...]
    all_to_all x1, blocking collectives: 11.3 us -> 9.87 us  [local(): lax.all_to_all(incoming, 'grp', split_axis=0, concat_axis=0, tiled=True)]
    convert_element_type x1, other arithmetic: 1.51 us -> 0.67 us  [local(): return sums[0].astype(BF16)]
    unnamed x2 -> x14, local copies, waits for them, and re-layouts: 0.66 us -> 0.05 us
  transfers between devices with their start and end apart: 4 -> 4, of which waited for: 3 -> 3; matrix products, arithmetic and copies ran while one was open for 0% -> 0% of each run, Pallas kernels for 5% -> 1%
where the time goes in v2:
time: 35.7 us; the launch traced here: 35.4 us
  waiting for transfers between devices  11 us (31%)
  blocking collectives  9.87 us (28%)
  starting transfers between devices  9.37 us (26%)
  Pallas kernels  3.64 us (10%)
  between operations  0.77 us (2%)
  other arithmetic  0.67 us (2%)
    all_to_all x1, blocking collectives, local(): lax.all_to_all(incoming, 'grp', split_axis=0, concat_axis=0, tiled=True)  9.87 us
    all_to_all x1, starting transfers between devices, local(): lax.all_to_all(outgoing, 'grp', split_axis=0, concat_axis=0, tiled=True)  7.45 us
    all_to_all x1, waiting for transfers between devices, local(): lax.all_to_all(outgoing, 'grp', split_axis=0, concat_axis=0, tiled=True)  7.07 us
    ppermute x3, waiting for transfers between devices, local(): sums.append(lax.ppermute(term, 'dir', pairs).astype(F32))  3.94 us
    pallas_call x1, Pallas kernels, local(): pl.pallas_call(functools.partial(project_kernel, readers, slots), out_sha...  1.96 us
    ppermute x3, starting transfers between devices, local(): sums.append(lax.ppermute(term, 'dir', pairs).astype(F32))  1.92 us
    pallas_call x1, Pallas kernels, local(): pl.pallas_call(functools.partial(translate_kernel, readers, slots, block)...  1.14 us
  transfers between devices with their start and end apart: 4, of which 3 were waited for; matrix products, arithmetic and copies ran while one was open for 0% of the time, Pallas kernels for 1%

profile of v2, /device:TPU:0, one launch (start us, length us, event | category | flops | bytes accessed | tf_op | source)
XLA Modules:
  0.0 35.4 jit_solution(10568578871207885184)
XLA Ops:
  0.7 2.0 %shard_map.137 = bf16[8,72,128]{2,1,0:T(8,128)(2,1)} custom-call(bf16[256,128]{1,0:T(8,128)(2,1)} %currents_hbm.1, s32[1,256]{1,0:T(1,128)} %bitcast.9, bf16[256,256]{1,0:T(8,128)(2,1)} %projection_ref.1, s32[16]{0:T(128)} %src_hbm.1, s32[16]{0:T(128)} %dst_hbm.1, s32[16]{0:T(128)} %type_hbm.1, s32[1,1]{1,0:T(1,128)} %bitcast.5.live_hbm, s32[8,8]{1,0:T(8,128)} %send_hbm.1, ...), custom_call_target="tpu_custom_call" | custom-call | tf_op jit(solution)/shard_map/pallas_call | solution.py:277
  2.6 0.0 copy-start.4
  2.6 0.0 copy-start.5
  2.6 0.0 copy-start.6
  2.7 0.0 copy-start.3
  2.7 7.5 %all-to-all-start = ((bf16[8,72,128]{2,1,0:T(8,128)(2,1)}), bf16[8,72,128]{2,1,0:T(8,128)(2,1)S(1)}, u32[]{:S(2)}, u32[]{:S(2)}) async-start(bf16[8,72,128]{2,1,0:T(8,128)(2,1)} %shard_map.137), calls=%async_computation | async-start | bytes 294912 | tf_op jit(solution)/shard_map/all_to_all | solution.py:286
  10.1 0.0 copy-done.4
  10.1 0.0 copy-done.5
  10.1 0.0 copy-done.6
  10.2 0.0 copy-start.1
  10.2 0.0 copy-start.2
  10.2 0.3 shard_map.136
  10.5 7.1 %all-to-all-done = bf16[8,72,128]{2,1,0:T(8,128)(2,1)S(1)} async-done(((bf16[8,72,128]{2,1,0:T(8,128)(2,1)}), bf16[8,72,128]{2,1,0:T(8,128)(2,1)S(1)}, u32[]{:S(2)}, u32[]{:S(2)}) %all-to-all-start) | async-done | bytes 147488 | tf_op jit(solution)/shard_map/all_to_all | solution.py:286
  17.6 0.0 copy-done.3
  17.6 0.0 copy-done.1
  17.6 0.0 copy-done.2
  17.6 1.1 %shard_map.138 = bf16[512,128]{1,0:T(8,128)(2,1)S(1)} custom-call(bf16[576,128]{1,0:T(8,128)(2,1)S(1)} %bitcast.6, f32[4,256,256]{2,1,0:T(8,128)S(1)} %get-tuple-element.8.response_ref, bf16[256,256]{1,0:T(8,128)(2,1)S(1)} %copy-done.1, bf16[256,128]{1,0:T(8,128)(2,1)S(1)} %copy-done.3, bf16[256,128]{1,0:T(8,128)(2,1)S(1)} %copy-done.2), custom_call_target="tpu_custom_call" | custom-call | tf_op jit(solution)/shard_map/pallas_call | solution.py:300
  18.7 0.0 copy-start
  18.8 9.9 %all_to_all.10 = bf16[8,64,128]{2,1,0:T(8,128)(2,1)S(1)} all-to-all(bf16[8,64,128]{2,1,0:T(8,128)(2,1)S(1)} %bitcast.7), channel_id=1, replica_groups=mesh['grp'=8,'dir'=4] {'grp'}, dimensions={0} | all-to-all | bytes 262144 | tf_op jit(solution)/shard_map/all_to_all | solution.py:320
  28.6 0.0 copy-done
  28.6 0.2 shard_map.139
  28.8 0.1 collective-permute-start.2
  28.9 1.6 %collective-permute-start.1 = (bf16[256,128]{1,0:T(8,128)(2,1)S(1)}, bf16[256,128]{1,0:T(8,128)(2,1)S(1)}, u32[]{:S(2)}, u32[]{:S(2)}) collective-permute-start(bf16[256,128]{1,0:T(8,128)(2,1)S(1)} %shard_map.139), channel_id=1, source_target_pairs={{0,2},{1,3},{2,0},{3,1},{4,6},{5,7},{6,4},{7,5},{8,10},{9,11},{10,... | collective-permute-start | bytes 196616 | tf_op jit(solution)/shard_map/ppermute | solution.py:332
  30.5 0.3 collective-permute-start
  30.8 2.5 %collective-permute-done.2 = bf16[256,128]{1,0:T(8,128)(2,1)S(1)} collective-permute-done((bf16[256,128]{1,0:T(8,128)(2,1)S(1)}, bf16[256,128]{1,0:T(8,128)(2,1)S(1)}, u32[]{:S(2)}, u32[]{:S(2)}) %collective-permute-start.2) | collective-permute-done | bytes 65568 | tf_op jit(solution)/shard_map/ppermute | solution.py:332
  33.3 1.4 %collective-permute-done.1 = bf16[256,128]{1,0:T(8,128)(2,1)S(1)} collective-permute-done((bf16[256,128]{1,0:T(8,128)(2,1)S(1)}, bf16[256,128]{1,0:T(8,128)(2,1)S(1)}, u32[]{:S(2)}, u32[]{:S(2)}) %collective-permute-start.1) | collective-permute-done | bytes 65568 | tf_op jit(solution)/shard_map/ppermute | solution.py:332
  34.7 0.0 collective-permute-done
  34.7 0.7 %add_convert_fusion = bf16[256,128]{1,0:T(8,128)(2,1)} fusion(bf16[256,128]{1,0:T(8,128)(2,1)S(1)} %collective-permute-done.2, bf16[256,128]{1,0:T(8,128)(2,1)S(1)} %collective-permute-done.1, bf16[256,128]{1,0:T(8,128)(2,1)S(1)} %collective-permute-done, bf16[256,128]{1,0:T(8,128)(2,1)S(1)} %shard_map.139), kind=kLoop, calls=%fused_computation | loop fusion | flops 262144 | bytes 327680 | tf_op jit(solution)/shard_map/convert_element_type | solution.py:335
Async XLA Ops:
  2.6 7.5 %copy-start.4 = (s32[256]{0:T(256)S(1)}, s32[256]{0:T(256)}, u32[]{:S(2)}) copy-start(s32[256]{0:T(256)} %param.15) | copy-start | bytes 3076
  2.6 7.5 %copy-start.5 = (bf16[4,64,256]{2,1,0:T(8,128)(2,1)S(1)}, bf16[4,64,256]{2,1,0:T(8,128)(2,1)}, u32[]{:S(2)}) copy-start(bf16[4,64,256]{2,1,0:T(8,128)(2,1)} %filters_ref.1) | copy-start | bytes 393220
  2.6 7.5 %copy-start.6 = (bf16[128,256]{1,0:T(8,128)(2,1)S(1)}, bf16[128,256]{1,0:T(8,128)(2,1)}, u32[]{:S(2)}) copy-start(bf16[128,256]{1,0:T(8,128)(2,1)} %constant.8.clone.wave_ref) | copy-start | bytes 196612
  2.7 14.9 %copy-start.3 = (bf16[256,128]{1,0:T(8,128)(2,1)S(1)}, bf16[256,128]{1,0:T(8,128)(2,1)}, u32[]{:S(2)}) copy-start(bf16[256,128]{1,0:T(8,128)(2,1)} %constant.10.clone.inverse_high_ref) | copy-start | bytes 196612
  2.7 14.9 %all-to-all-start = ((bf16[8,72,128]{2,1,0:T(8,128)(2,1)}), bf16[8,72,128]{2,1,0:T(8,128)(2,1)S(1)}, u32[]{:S(2)}, u32[]{:S(2)}) async-start(bf16[8,72,128]{2,1,0:T(8,128)(2,1)} %shard_map.137), calls=%async_computation | async-start | bytes 294912 | tf_op jit(solution)/shard_map/all_to_all | solution.py:286
  10.2 7.4 %copy-start.1 = (bf16[256,256]{1,0:T(8,128)(2,1)S(1)}, bf16[256,256]{1,0:T(8,128)(2,1)}, u32[]{:S(2)}) copy-start(bf16[256,256]{1,0:T(8,128)(2,1)} %constant.9.clone.forward_ref) | copy-start | bytes 393220
  10.2 7.4 %copy-start.2 = (bf16[256,128]{1,0:T(8,128)(2,1)S(1)}, bf16[256,128]{1,0:T(8,128)(2,1)}, u32[]{:S(2)}) copy-start(bf16[256,128]{1,0:T(8,128)(2,1)} %constant.11.clone.inverse_low_ref) | copy-start | bytes 196612
  18.7 9.9 %copy-start = (bf16[256,256]{1,0:T(8,128)(2,1)S(1)}, bf16[256,256]{1,0:T(8,128)(2,1)}, u32[]{:S(2)}) copy-start(bf16[256,256]{1,0:T(8,128)(2,1)} %projection_ref.1) | copy-start | bytes 393220
  28.8 4.4 %collective-permute-start.2 = (bf16[256,128]{1,0:T(8,128)(2,1)S(1)}, bf16[256,128]{1,0:T(8,128)(2,1)S(1)}, u32[]{:S(2)}, u32[]{:S(2)}) collective-permute-start(bf16[256,128]{1,0:T(8,128)(2,1)S(1)} %shard_map.139), channel_id=1, source_target_pairs={{0,3},{1,2},{2,1},{3,0},{4,7},{5,6},{6,5},{7,4},{8,11},{9,10},{10,... | collective-permute-start | bytes 196616 | tf_op jit(solution)/shard_map/ppermute | solution.py:332
  28.9 5.8 %collective-permute-start.1 = (bf16[256,128]{1,0:T(8,128)(2,1)S(1)}, bf16[256,128]{1,0:T(8,128)(2,1)S(1)}, u32[]{:S(2)}, u32[]{:S(2)}) collective-permute-start(bf16[256,128]{1,0:T(8,128)(2,1)S(1)} %shard_map.139), channel_id=1, source_target_pairs={{0,2},{1,3},{2,0},{3,1},{4,6},{5,7},{6,4},{7,5},{8,10},{9,11},{10,... | collective-permute-start | bytes 196616 | tf_op jit(solution)/shard_map/ppermute | solution.py:332
  30.5 4.2 %collective-permute-start = (bf16[256,128]{1,0:T(8,128)(2,1)S(1)}, bf16[256,128]{1,0:T(8,128)(2,1)S(1)}, u32[]{:S(2)}, u32[]{:S(2)}) collective-permute-start(bf16[256,128]{1,0:T(8,128)(2,1)S(1)} %shard_map.139), channel_id=1, source_target_pairs={{0,1},{1,0},{2,3},{3,2},{4,5},{5,4},{6,7},{7,6},{8,9},{9,8},{10,11... | collective-permute-start | bytes 196616 | tf_op jit(solution)/shard_map/ppermute | solution.py:332

commit v3 on v2

--- a/solution.py
+++ b/solution.py
@@ -216,27 +216,40 @@
     result_ref[...] = (
         dot(high, inverse_high) + dot(low, inverse_high) + dot(high, inverse_low_ref[...])
     )
+    copies = out_ref.shape[0] // (groups * block)
     for g in range(groups):
-        out_ref[pl.ds(g * block, block), :] = result_ref[
-            pl.ds(g, block, stride=groups), :
-        ].astype(BF16)
-
-
-def field_kernel(readers, block, column_ref, projection_ref, incoming_ref, out_ref):
+        part = result_ref[pl.ds(g, block, stride=groups), :].astype(BF16)
+        owner, own = divmod(g, G_DEV)
+        for copy in range(copies):
+            start = ((copy * readers + owner) * G_DEV + own) * block
+            out_ref[pl.ds(start, block), :] = part
+
+
+def field_kernel(readers, block, column_ref, own_ref, other_ref, incoming_ref, out_ref):
     column = column_ref[:, :1]
-    projection = projection_ref[...]
+    outer = lax.axis_size("outer")
+    here = lax.axis_index("outer")
+    own = own_ref[...]
+    if outer == 1:
+        projection = own
+    else:
+        other = other_ref[...]
+        projection = jnp.concatenate(
+            [jnp.where(here == x, own, other) for x in range(outer)], axis=1
+        )
     field = None
     for g in range(G_DEV):
         incoming = jnp.concatenate(
             [
-                incoming_ref[pl.ds((part * G_DEV + g) * block, block), :]
+                incoming_ref[pl.ds(((x * readers + part) * G_DEV + g) * block, block), :]
+                for x in range(outer)
                 for part in range(readers)
             ],
             axis=0,
         )
         term = dot(projection, incoming)
         field = term if g == 0 else jnp.where(column == g, term, field)
-    out_ref[...] = field.astype(BF16)
+    out_ref[...] = field
 
 
 def local(
@@ -252,7 +265,8 @@
     recv_group,
 ):
     readers = lax.axis_size("grp")
-    spans = lax.axis_size("dir")
+    outer = lax.axis_size("outer")
+    inner = lax.axis_size("inner")
     steps = currents.shape[1]
     basis, width = projection.shape
     types, taps, _ = filters.shape
@@ -284,6 +298,7 @@
         + [pltpu.SemaphoreType.DMA((len(inputs),))],
     )(*inputs)
     arrived = lax.all_to_all(outgoing, "grp", split_axis=0, concat_axis=0, tiled=True)
+    partner = lax.ppermute(projection, "outer", [(0, 1), (1, 0)])
     response, column = pl.pallas_call(
         filter_kernel,
         out_shape=(
@@ -297,9 +312,10 @@
             flops=8 * types * width * taps * steps, bytes_accessed=2**21, transcendentals=0
         ),
     )(group_row, filters, np.concatenate([forward_high[:taps], forward_low[:taps]], axis=0))
+    arrived, partner = lax.optimization_barrier((arrived, partner))
     incoming = pl.pallas_call(
         functools.partial(translate_kernel, readers, slots, block),
-        out_shape=pltpu.VMEM((groups * block, steps), BF16),
+        out_shape=pltpu.VMEM((outer * groups * block, steps), BF16),
         in_specs=[VMEM, VMEM, VMEM, VMEM, VMEM],
         out_specs=VMEM,
         compiler_params=PARAMS,
@@ -316,34 +332,39 @@
         near(jnp.asarray(inverse_high)),
         near(jnp.asarray(inverse_low)),
     )
-    incoming = incoming.reshape(readers, G_DEV * block, steps)
-    own = lax.all_to_all(incoming, "grp", split_axis=0, concat_axis=0, tiled=True)
+    incoming = incoming.reshape(outer * readers, G_DEV * block, steps)
+    own = lax.all_to_all(incoming, ("outer", "grp"), split_axis=0, concat_axis=0, tiled=True)
     term = pl.pallas_call(
         functools.partial(field_kernel, readers, block),
-        out_shape=pltpu.VMEM((basis, steps), BF16),
-        in_specs=[VMEM, VMEM, VMEM],
+        out_shape=pltpu.VMEM((basis, steps), F32),
+        in_specs=[VMEM, VMEM, VMEM, VMEM],
         out_specs=VMEM,
         compiler_params=PARAMS,
-    )(near(column), near(projection), near(own.reshape(groups * block, steps)))
-
-    sums = [term.astype(F32)]
-    for other in range(1, spans):
-        pairs = [(d, d ^ other) for d in range(spans)]
-        sums.append(lax.ppermute(term, "dir", pairs).astype(F32))
-    while len(sums) > 1:
-        sums = [sums[i] + sums[i + 1] for i in range(0, len(sums), 2)]
-    return sums[0].astype(BF16)
+    )(
+        near(column),
+        near(projection),
+        near(partner),
+        near(own.reshape(outer * groups * block, steps)),
+    )
+    total = term
+    if inner > 1:
+        total = term + lax.ppermute(term, "inner", [(0, 1), (1, 0)])
+    return total.astype(BF16)
 
 
 def solution(mesh):
+    readers, spans = mesh.devices.shape
+    split_mesh = jax.sharding.Mesh(
+        mesh.devices.reshape(readers, spans // 2, 2), ("grp", "outer", "inner")
+    )
     return jax.shard_map(
         local,
-        mesh=mesh,
+        mesh=split_mesh,
         in_specs=(
             P("grp", None),
             P("grp"),
-            P("grp", "dir"),
-            P(None, None, "dir"),
+            P("grp", ("outer", "inner")),
+            P(None, None, ("outer", "inner")),
             P("grp"),
             P("grp"),
             P("grp"),

time: 35.7 us -> 34.3 us (0.961)
  waiting for transfers between devices: 11 us -> 6.87 us
  blocking collectives: 9.87 us -> 12.9 us
    all_to_all x1, waiting for transfers between devices: 7.07 us -> 2.39 us  [local(): lax.all_to_all(outgoing, 'grp', split_axis=0, concat_axis=0, tiled=True)]
    all_to_all x1, blocking collectives: 9.87 us -> 12.9 us  [local(): lax.all_to_all(incoming, ('outer', 'grp'), split_axis=0, concat_axis=0, t...]
    ppermute x3 -> x2, waiting for transfers between devices: 3.94 us -> 4.48 us  [the longest x1 3.14 us: local(): partner = lax.ppermute(projection, 'outer', [(0, 1), (1, 0)])]
    ppermute x3 -> x2, starting transfers between devices: 1.92 us -> 1.63 us  [the longest x1 1.55 us: local(): partner = lax.ppermute(projection, 'outer', [(0, 1), (1, 0)])]
  transfers between devices with their start and end apart: 4 -> 3, of which waited for: 3 -> 3; matrix products, arithmetic and copies ran while one was open for 0% -> 0% of each run, Pallas kernels for 1% -> 1%
where the time goes in v3:
time: 34.3 us; the launch traced here: 34 us
  blocking collectives  12.9 us (38%)
  starting transfers between devices  9.08 us (26%)
  waiting for transfers between devices  6.87 us (20%)
  Pallas kernels  3.7 us (11%)
  between operations  0.75 us (2%)
  other arithmetic  0.65 us (2%)
    all_to_all x1, blocking collectives, local(): lax.all_to_all(incoming, ('outer', 'grp'), split_axis=0, concat_axis=0, t...  12.9 us
    all_to_all x1, starting transfers between devices, local(): lax.all_to_all(outgoing, 'grp', split_axis=0, concat_axis=0, tiled=True)  7.45 us
    ppermute x1, waiting for transfers between devices, local(): partner = lax.ppermute(projection, 'outer', [(0, 1), (1, 0)])  3.14 us
    all_to_all x1, waiting for transfers between devices, local(): lax.all_to_all(outgoing, 'grp', split_axis=0, concat_axis=0, tiled=True)  2.39 us
    pallas_call x1, Pallas kernels, local(): pl.pallas_call(functools.partial(project_kernel, readers, slots), out_sha...  1.95 us
    ppermute x1, starting transfers between devices, local(): partner = lax.ppermute(projection, 'outer', [(0, 1), (1, 0)])  1.55 us
    ppermute x1, waiting for transfers between devices, local(): total = term + lax.ppermute(term, 'inner', [(0, 1), (1, 0)])  1.33 us
    pallas_call x1, Pallas kernels, local(): pl.pallas_call(functools.partial(translate_kernel, readers, slots, block)...  1.14 us
  transfers between devices with their start and end apart: 3, of which 3 were waited for; matrix products, arithmetic and copies ran while one was open for 0% of the time, Pallas kernels for 1%

profile of v3, /device:TPU:0, one launch (start us, length us, event | category | flops | bytes accessed | tf_op | source)
XLA Modules:
  0.0 34.0 jit_solution(5346991727767333625)
XLA Ops:
  0.7 0.0 copy-start.5
  0.7 2.0 %shard_map.137 = bf16[8,72,128]{2,1,0:T(8,128)(2,1)} custom-call(bf16[256,128]{1,0:T(8,128)(2,1)} %currents_hbm.1, s32[1,256]{1,0:T(1,128)} %bitcast.9, bf16[256,256]{1,0:T(8,128)(2,1)} %own_ref.1, s32[16]{0:T(128)} %src_hbm.1, s32[16]{0:T(128)} %dst_hbm.1, s32[16]{0:T(128)} %type_hbm.1, s32[1,1]{1,0:T(1,128)} %bitcast.5.live_hbm, s32[8,8]{1,0:T(8,128)} %send_hbm.1, ...), custom_call_target="tpu_custom_call" | custom-call | tf_op jit(solution)/shard_map/pallas_call | solution.py:291
  2.6 0.0 copy-start
  2.6 0.0 copy-start.4
  2.6 0.0 copy-start.6
  2.7 0.0 copy-start.3
  2.7 7.5 %all-to-all-start = ((bf16[8,72,128]{2,1,0:T(8,128)(2,1)}), bf16[8,72,128]{2,1,0:T(8,128)(2,1)S(1)}, u32[]{:S(2)}, u32[]{:S(2)}) async-start(bf16[8,72,128]{2,1,0:T(8,128)(2,1)} %shard_map.137), calls=%async_computation | async-start | bytes 294912 | tf_op jit(solution)/shard_map/all_to_all | solution.py:300
  10.1 0.0 copy-done
  10.1 0.0 copy-start.1
  10.1 0.0 copy-start.2
  10.2 1.6 %collective-permute-start = (bf16[256,256]{1,0:T(8,128)(2,1)S(1)}, bf16[256,256]{1,0:T(8,128)(2,1)S(1)}, u32[]{:S(2)}, u32[]{:S(2)}) collective-permute-start(bf16[256,256]{1,0:T(8,128)(2,1)S(1)} %copy-done), channel_id=1, source_target_pairs={{0,2},{2,0},{1,3},{3,1},{4,6},{6,4},{5,7},{7,5},{8,10},{10,8},{9,1... | collective-permute-start | bytes 393224 | tf_op jit(solution)/shard_map/ppermute | solution.py:301
  11.7 0.0 copy-done.5
  11.7 0.0 copy-done.4
  11.7 0.0 copy-done.6
  11.7 0.3 shard_map.136
  12.0 3.1 %collective-permute-done.other_ref = bf16[256,256]{1,0:T(8,128)(2,1)S(1)} collective-permute-done((bf16[256,256]{1,0:T(8,128)(2,1)S(1)}, bf16[256,256]{1,0:T(8,128)(2,1)S(1)}, u32[]{:S(2)}, u32[]{:S(2)}) %collective-permute-start) | collective-permute-done | bytes 131104 | tf_op jit(solution)/shard_map/ppermute | solution.py:301
  15.2 2.4 %all-to-all-done = bf16[8,72,128]{2,1,0:T(8,128)(2,1)S(1)} async-done(((bf16[8,72,128]{2,1,0:T(8,128)(2,1)}), bf16[8,72,128]{2,1,0:T(8,128)(2,1)S(1)}, u32[]{:S(2)}, u32[]{:S(2)}) %all-to-all-start) | async-done | bytes 147488 | tf_op jit(solution)/shard_map/all_to_all | solution.py:300
  17.6 0.0 copy-done.3
  17.6 0.0 copy-done.1
  17.6 0.0 copy-done.2
  17.6 1.1 %shard_map.138 = bf16[1024,128]{1,0:T(8,128)(2,1)S(1)} custom-call(bf16[576,128]{1,0:T(8,128)(2,1)S(1)} %bitcast.8, f32[4,256,256]{2,1,0:T(8,128)S(1)} %get-tuple-element.12.response_ref, bf16[256,256]{1,0:T(8,128)(2,1)S(1)} %copy-done.1, bf16[256,128]{1,0:T(8,128)(2,1)S(1)} %copy-done.3, bf16[256,128]{1,0:T(8,128)(2,1)S(1)} %copy-done.2), custom_call_target="tpu_custom_call" | custom-call | tf_op jit(solution)/shard_map/pallas_call | solution.py:316
  18.7 12.9 %all_to_all.10 = bf16[16,64,128]{2,1,0:T(8,128)(2,1)S(1)} all-to-all(bf16[16,64,128]{2,1,0:T(8,128)(2,1)S(1)} %bitcast.7), channel_id=1, replica_groups=mesh['grp'=8,'outer'=2,'inner'=2] {'outer','grp'}, dimensions={0} | all-to-all | bytes 524288 | tf_op jit(solution)/shard_map/all_to_all | solution.py:336
  31.6 0.3 shard_map.139
  31.9 0.1 collective-permute-start.1
  32.0 1.3 %collective-permute-done.1 = f32[256,128]{1,0:T(8,128)S(1)} collective-permute-done((f32[256,128]{1,0:T(8,128)S(1)}, f32[256,128]{1,0:T(8,128)S(1)}, u32[]{:S(2)}, u32[]{:S(2)}) %collective-permute-start.1) | collective-permute-done | bytes 131104 | tf_op jit(solution)/shard_map/ppermute | solution.py:351
  33.4 0.7 %add_convert_fusion = bf16[256,128]{1,0:T(8,128)(2,1)} fusion(f32[256,128]{1,0:T(8,128)S(1)} %shard_map.139, f32[256,128]{1,0:T(8,128)S(1)} %collective-permute-done.1), kind=kLoop, calls=%fused_computation | loop fusion | flops 65536 | bytes 327680 | tf_op jit(solution)/shard_map/convert_element_type | solution.py:352
Async XLA Ops:
  0.7 11.1 %copy-start.5 = (bf16[4,64,256]{2,1,0:T(8,128)(2,1)S(1)}, bf16[4,64,256]{2,1,0:T(8,128)(2,1)}, u32[]{:S(2)}) copy-start(bf16[4,64,256]{2,1,0:T(8,128)(2,1)} %filters_ref.1) | copy-start | bytes 393220
  2.6 7.5 %copy-start = (bf16[256,256]{1,0:T(8,128)(2,1)S(1)}, bf16[256,256]{1,0:T(8,128)(2,1)}, u32[]{:S(2)}) copy-start(bf16[256,256]{1,0:T(8,128)(2,1)} %own_ref.1) | copy-start | bytes 393220
  2.6 9.1 %copy-start.4 = (s32[256]{0:T(256)S(1)}, s32[256]{0:T(256)}, u32[]{:S(2)}) copy-start(s32[256]{0:T(256)} %param.15) | copy-start | bytes 3076
  2.6 9.1 %copy-start.6 = (bf16[128,256]{1,0:T(8,128)(2,1)S(1)}, bf16[128,256]{1,0:T(8,128)(2,1)}, u32[]{:S(2)}) copy-start(bf16[128,256]{1,0:T(8,128)(2,1)} %constant.8.clone.wave_ref) | copy-start | bytes 196612
  2.7 14.9 %copy-start.3 = (bf16[256,128]{1,0:T(8,128)(2,1)S(1)}, bf16[256,128]{1,0:T(8,128)(2,1)}, u32[]{:S(2)}) copy-start(bf16[256,128]{1,0:T(8,128)(2,1)} %constant.10.clone.inverse_high_ref) | copy-start | bytes 196612
  2.7 14.9 %all-to-all-start = ((bf16[8,72,128]{2,1,0:T(8,128)(2,1)}), bf16[8,72,128]{2,1,0:T(8,128)(2,1)S(1)}, u32[]{:S(2)}, u32[]{:S(2)}) async-start(bf16[8,72,128]{2,1,0:T(8,128)(2,1)} %shard_map.137), calls=%async_computation | async-start | bytes 294912 | tf_op jit(solution)/shard_map/all_to_all | solution.py:300
  10.1 7.5 %copy-start.1 = (bf16[256,256]{1,0:T(8,128)(2,1)S(1)}, bf16[256,256]{1,0:T(8,128)(2,1)}, u32[]{:S(2)}) copy-start(bf16[256,256]{1,0:T(8,128)(2,1)} %constant.9.clone.forward_ref) | copy-start | bytes 393220
  10.1 7.4 %copy-start.2 = (bf16[256,128]{1,0:T(8,128)(2,1)S(1)}, bf16[256,128]{1,0:T(8,128)(2,1)}, u32[]{:S(2)}) copy-start(bf16[256,128]{1,0:T(8,128)(2,1)} %constant.11.clone.inverse_low_ref) | copy-start | bytes 196612
  10.2 5.0 %collective-permute-start = (bf16[256,256]{1,0:T(8,128)(2,1)S(1)}, bf16[256,256]{1,0:T(8,128)(2,1)S(1)}, u32[]{:S(2)}, u32[]{:S(2)}) collective-permute-start(bf16[256,256]{1,0:T(8,128)(2,1)S(1)} %copy-done), channel_id=1, source_target_pairs={{0,2},{2,0},{1,3},{3,1},{4,6},{6,4},{5,7},{7,5},{8,10},{10,8},{9,1... | collective-permute-start | bytes 393224 | tf_op jit(solution)/shard_map/ppermute | solution.py:301
  31.9 1.4 %collective-permute-start.1 = (f32[256,128]{1,0:T(8,128)S(1)}, f32[256,128]{1,0:T(8,128)S(1)}, u32[]{:S(2)}, u32[]{:S(2)}) collective-permute-start(f32[256,128]{1,0:T(8,128)S(1)} %shard_map.139), channel_id=1, source_target_pairs={{0,1},{1,0},{2,3},{3,2},{4,5},{5,4},{6,7},{7,6},{8,9},{9,8},{10,11... | collective-permute-start | bytes 393224 | tf_op jit(solution)/shard_map/ppermute | solution.py:351

commit v4 on v3

--- a/solution.py
+++ b/solution.py
@@ -1,4 +1,5 @@
 import functools
+import math
 
 import jax
 import jax.numpy as jnp
@@ -166,8 +167,10 @@
         part = arrived_ref[pl.ds(owner * rows, G_DEV * block), :]
         order_ref[pl.ds(owner * G_DEV * block, G_DEV * block), :] = part.astype(F32)
 
+    chunk = math.gcd(block, max(1, LANES // groups))
+    span = chunk * groups
     pack = max(1, LANES // slots)
-    count = jnp.zeros((types * groups, groups), F32)
+    count = jnp.zeros((types * groups, 2 * span), F32)
     bucket_row = lax.broadcasted_iota(jnp.int32, (types * groups, LANES), 0)
     group_row = lax.broadcasted_iota(jnp.int32, (groups, LANES), 0)
     for first in range(0, readers, pack):
@@ -180,45 +183,51 @@
         bucket = jnp.where(target > 0, kind * groups + target - 1, -1)
         to_bucket = (bucket_row == bucket).astype(F32).astype(BF16)
         from_group = (group_row == source).astype(F32).astype(BF16)
+        from_group = jnp.concatenate([from_group] * (2 * chunk), axis=0)
         count = count + dot(to_bucket, from_group, ((1,), (1,)))
-    count_high, count_low = split(count)
-    if readers * slots > 256:
-        count_parts = jnp.concatenate([count_high, count_high, count_low, count_low], axis=1)
-    else:
-        count_parts = jnp.concatenate([count_high, count_high], axis=1)
+    column = lax.broadcasted_iota(jnp.int32, (1, 2 * span), 1)
+    column = jnp.where(column >= span, column - span, column)
+    counts = []
+    for i in range(chunk):
+        own = (column >= i * groups) & (column < (i + 1) * groups)
+        counts.append(count * own.astype(F32))
+    counts = split(jnp.concatenate(counts, axis=0))
+    if readers * slots <= 256:
+        counts = counts[:1]
 
     forward = forward_ref[...]
-    for k in range(block):
-        signal = order_ref[pl.ds(k, groups, stride=block), :].astype(BF16)
-        wave_ref[pl.ds(k * groups, groups), :] = signal
-    signals = wave_ref[...]
+    signals = order_ref[...].reshape(groups, block, steps)
+    signals = jnp.swapaxes(signals, 0, 1).reshape(groups * block, steps).astype(BF16)
     waves = dot(jnp.concatenate([signals, signals], axis=1), forward)
-    for k in range(block):
-        high, low = split(waves[k * groups : (k + 1) * groups])
-        if readers * slots > 256:
-            parts = jnp.concatenate([high, low, high, low], axis=0)
-        else:
-            parts = jnp.concatenate([high, low], axis=0)
-        gathered = dot(count_parts, parts)
-        real = jnp.zeros((groups, steps), F32)
-        imag = jnp.zeros((groups, steps), F32)
-        for c in range(types):
-            response = response_ref[c, pl.ds(base + k, 1), :]
-            response_real, response_imag = response[:, :steps], response[:, steps:]
-            bucket = gathered[c * groups : (c + 1) * groups]
-            bucket_real, bucket_imag = bucket[:, :steps], bucket[:, steps:]
-            real = real + (bucket_real * response_real - bucket_imag * response_imag)
-            imag = imag + (bucket_real * response_imag + bucket_imag * response_real)
-        product_ref[pl.ds(k * groups, groups), pl.ds(0, steps)] = real
-        product_ref[pl.ds(k * groups, groups), pl.ds(steps, steps)] = imag
+    for first in range(0, block, chunk):
+        parts = jnp.concatenate(split(waves[first * groups : first * groups + span]), axis=0)
+        gathered = dot(counts[0], parts)
+        for extra in counts[1:]:
+            gathered = gathered + dot(extra, parts)
+        for i in range(chunk):
+            k = first + i
+            real = imag = None
+            for c in range(types):
+                response = response_ref[c, pl.ds(base + k, 1), :]
+                response_real, response_imag = response[:, :steps], response[:, steps:]
+                start = (i * types + c) * groups
+                bucket = gathered[start : start + groups]
+                bucket_real, bucket_imag = bucket[:, :steps], bucket[:, steps:]
+                term_real = bucket_real * response_real - bucket_imag * response_imag
+                term_imag = bucket_real * response_imag + bucket_imag * response_real
+                real = term_real if c == 0 else real + term_real
+                imag = term_imag if c == 0 else imag + term_imag
+            product_ref[pl.ds(k * groups, groups), pl.ds(0, steps)] = real
+            product_ref[pl.ds(k * groups, groups), pl.ds(steps, steps)] = imag
     high, low = split(product_ref[...])
     inverse_high = inverse_high_ref[...]
-    result_ref[...] = (
-        dot(high, inverse_high) + dot(low, inverse_high) + dot(high, inverse_low_ref[...])
-    )
+    both = dot(high, jnp.concatenate([inverse_high, inverse_low_ref[...]], axis=1))
+    result_ref[...] = both[:, :steps] + both[:, steps:] + dot(low, inverse_high)
     copies = out_ref.shape[0] // (groups * block)
+    result = jnp.swapaxes(result_ref[...].reshape(block, groups, steps), 0, 1)
+    result = result.reshape(groups * block, steps).astype(BF16)
     for g in range(groups):
-        part = result_ref[pl.ds(g, block, stride=groups), :].astype(BF16)
+        part = result[g * block : (g + 1) * block]
         owner, own = divmod(g, G_DEV)
         for copy in range(copies):
             start = ((copy * readers + owner) * G_DEV + own) * block

time: 34.3 us -> 34 us (level)
  no operation moved by 1% of the time
where the time goes in v4:
time: 34 us; the launch traced here: 33.7 us
  blocking collectives  12.9 us (38%)
  starting transfers between devices  9.08 us (27%)
  waiting for transfers between devices  6.87 us (20%)
  Pallas kernels  3.45 us (10%)
  between operations  0.75 us (2%)
  other arithmetic  0.65 us (2%)
    all_to_all x1, blocking collectives, local(): lax.all_to_all(incoming, ('outer', 'grp'), split_axis=0, concat_axis=0, t...  12.9 us
    all_to_all x1, starting transfers between devices, local(): lax.all_to_all(outgoing, 'grp', split_axis=0, concat_axis=0, tiled=True)  7.45 us
    ppermute x1, waiting for transfers between devices, local(): partner = lax.ppermute(projection, 'outer', [(0, 1), (1, 0)])  3.14 us
    all_to_all x1, waiting for transfers between devices, local(): lax.all_to_all(outgoing, 'grp', split_axis=0, concat_axis=0, tiled=True)  2.39 us
    pallas_call x1, Pallas kernels, local(): pl.pallas_call(functools.partial(project_kernel, readers, slots), out_sha...  1.95 us
    ppermute x1, starting transfers between devices, local(): partner = lax.ppermute(projection, 'outer', [(0, 1), (1, 0)])  1.55 us
    ppermute x1, waiting for transfers between devices, local(): total = term + lax.ppermute(term, 'inner', [(0, 1), (1, 0)])  1.33 us
    pallas_call x1, Pallas kernels, local(): pl.pallas_call(functools.partial(translate_kernel, readers, slots, block)...  0.89 us
  transfers between devices with their start and end apart: 3, of which 3 were waited for; matrix products, arithmetic and copies ran while one was open for 0% of the time, Pallas kernels for 1%

profile of v4, /device:TPU:0, one launch (start us, length us, event | category | flops | bytes accessed | tf_op | source)
XLA Modules:
  0.0 33.7 jit_solution(6960692151972031372)
XLA Ops:
  0.7 0.0 copy-start.5
  0.7 2.0 %shard_map.137 = bf16[8,72,128]{2,1,0:T(8,128)(2,1)} custom-call(bf16[256,128]{1,0:T(8,128)(2,1)} %currents_hbm.1, s32[1,256]{1,0:T(1,128)} %bitcast.9, bf16[256,256]{1,0:T(8,128)(2,1)} %own_ref.1, s32[16]{0:T(128)} %src_hbm.1, s32[16]{0:T(128)} %dst_hbm.1, s32[16]{0:T(128)} %type_hbm.1, s32[1,1]{1,0:T(1,128)} %bitcast.5.live_hbm, s32[8,8]{1,0:T(8,128)} %send_hbm.1, ...), custom_call_target="tpu_custom_call" | custom-call | tf_op jit(solution)/shard_map/pallas_call | solution.py:300
  2.6 0.0 copy-start
  2.6 0.0 copy-start.4
  2.6 0.0 copy-start.6
  2.7 0.0 copy-start.3
  2.7 7.5 %all-to-all-start = ((bf16[8,72,128]{2,1,0:T(8,128)(2,1)}), bf16[8,72,128]{2,1,0:T(8,128)(2,1)S(1)}, u32[]{:S(2)}, u32[]{:S(2)}) async-start(bf16[8,72,128]{2,1,0:T(8,128)(2,1)} %shard_map.137), calls=%async_computation | async-start | bytes 294912 | tf_op jit(solution)/shard_map/all_to_all | solution.py:309
  10.1 0.0 copy-done
  10.1 0.0 copy-start.1
  10.1 0.0 copy-start.2
  10.2 1.6 %collective-permute-start = (bf16[256,256]{1,0:T(8,128)(2,1)S(1)}, bf16[256,256]{1,0:T(8,128)(2,1)S(1)}, u32[]{:S(2)}, u32[]{:S(2)}) collective-permute-start(bf16[256,256]{1,0:T(8,128)(2,1)S(1)} %copy-done), channel_id=1, source_target_pairs={{0,2},{2,0},{1,3},{3,1},{4,6},{6,4},{5,7},{7,5},{8,10},{10,8},{9,1... | collective-permute-start | bytes 393224 | tf_op jit(solution)/shard_map/ppermute | solution.py:310
  11.7 0.0 copy-done.5
  11.7 0.0 copy-done.4
  11.7 0.0 copy-done.6
  11.7 0.3 shard_map.136
  12.0 3.1 %collective-permute-done.other_ref = bf16[256,256]{1,0:T(8,128)(2,1)S(1)} collective-permute-done((bf16[256,256]{1,0:T(8,128)(2,1)S(1)}, bf16[256,256]{1,0:T(8,128)(2,1)S(1)}, u32[]{:S(2)}, u32[]{:S(2)}) %collective-permute-start) | collective-permute-done | bytes 131104 | tf_op jit(solution)/shard_map/ppermute | solution.py:310
  15.2 2.4 %all-to-all-done = bf16[8,72,128]{2,1,0:T(8,128)(2,1)S(1)} async-done(((bf16[8,72,128]{2,1,0:T(8,128)(2,1)}), bf16[8,72,128]{2,1,0:T(8,128)(2,1)S(1)}, u32[]{:S(2)}, u32[]{:S(2)}) %all-to-all-start) | async-done | bytes 147488 | tf_op jit(solution)/shard_map/all_to_all | solution.py:309
  17.6 0.0 copy-done.3
  17.6 0.0 copy-done.1
  17.6 0.0 copy-done.2
  17.6 0.9 %shard_map.138 = bf16[1024,128]{1,0:T(8,128)(2,1)S(1)} custom-call(bf16[576,128]{1,0:T(8,128)(2,1)S(1)} %bitcast.8, f32[4,256,256]{2,1,0:T(8,128)S(1)} %get-tuple-element.12.response_ref, bf16[256,256]{1,0:T(8,128)(2,1)S(1)} %copy-done.1, bf16[256,128]{1,0:T(8,128)(2,1)S(1)} %copy-done.3, bf16[256,128]{1,0:T(8,128)(2,1)S(1)} %copy-done.2), custom_call_target="tpu_custom_call" | custom-call | tf_op jit(solution)/shard_map/pallas_call | solution.py:325
  18.5 12.9 %all_to_all.10 = bf16[16,64,128]{2,1,0:T(8,128)(2,1)S(1)} all-to-all(bf16[16,64,128]{2,1,0:T(8,128)(2,1)S(1)} %bitcast.7), channel_id=1, replica_groups=mesh['grp'=8,'outer'=2,'inner'=2] {'outer','grp'}, dimensions={0} | all-to-all | bytes 524288 | tf_op jit(solution)/shard_map/all_to_all | solution.py:345
  31.4 0.3 shard_map.139
  31.7 0.1 collective-permute-start.1
  31.8 1.3 %collective-permute-done.1 = f32[256,128]{1,0:T(8,128)S(1)} collective-permute-done((f32[256,128]{1,0:T(8,128)S(1)}, f32[256,128]{1,0:T(8,128)S(1)}, u32[]{:S(2)}, u32[]{:S(2)}) %collective-permute-start.1) | collective-permute-done | bytes 131104 | tf_op jit(solution)/shard_map/ppermute | solution.py:360
  33.1 0.7 %add_convert_fusion = bf16[256,128]{1,0:T(8,128)(2,1)} fusion(f32[256,128]{1,0:T(8,128)S(1)} %shard_map.139, f32[256,128]{1,0:T(8,128)S(1)} %collective-permute-done.1), kind=kLoop, calls=%fused_computation | loop fusion | flops 65536 | bytes 327680 | tf_op jit(solution)/shard_map/convert_element_type | solution.py:361
Async XLA Ops:
  0.7 11.1 %copy-start.5 = (bf16[4,64,256]{2,1,0:T(8,128)(2,1)S(1)}, bf16[4,64,256]{2,1,0:T(8,128)(2,1)}, u32[]{:S(2)}) copy-start(bf16[4,64,256]{2,1,0:T(8,128)(2,1)} %filters_ref.1) | copy-start | bytes 393220
  2.6 7.5 %copy-start = (bf16[256,256]{1,0:T(8,128)(2,1)S(1)}, bf16[256,256]{1,0:T(8,128)(2,1)}, u32[]{:S(2)}) copy-start(bf16[256,256]{1,0:T(8,128)(2,1)} %own_ref.1) | copy-start | bytes 393220
  2.6 9.1 %copy-start.4 = (s32[256]{0:T(256)S(1)}, s32[256]{0:T(256)}, u32[]{:S(2)}) copy-start(s32[256]{0:T(256)} %param.15) | copy-start | bytes 3076
  2.6 9.1 %copy-start.6 = (bf16[128,256]{1,0:T(8,128)(2,1)S(1)}, bf16[128,256]{1,0:T(8,128)(2,1)}, u32[]{:S(2)}) copy-start(bf16[128,256]{1,0:T(8,128)(2,1)} %constant.8.clone.wave_ref) | copy-start | bytes 196612
  2.7 14.9 %copy-start.3 = (bf16[256,128]{1,0:T(8,128)(2,1)S(1)}, bf16[256,128]{1,0:T(8,128)(2,1)}, u32[]{:S(2)}) copy-start(bf16[256,128]{1,0:T(8,128)(2,1)} %constant.10.clone.inverse_high_ref) | copy-start | bytes 196612
  2.7 14.9 %all-to-all-start = ((bf16[8,72,128]{2,1,0:T(8,128)(2,1)}), bf16[8,72,128]{2,1,0:T(8,128)(2,1)S(1)}, u32[]{:S(2)}, u32[]{:S(2)}) async-start(bf16[8,72,128]{2,1,0:T(8,128)(2,1)} %shard_map.137), calls=%async_computation | async-start | bytes 294912 | tf_op jit(solution)/shard_map/all_to_all | solution.py:309
  10.1 7.5 %copy-start.1 = (bf16[256,256]{1,0:T(8,128)(2,1)S(1)}, bf16[256,256]{1,0:T(8,128)(2,1)}, u32[]{:S(2)}) copy-start(bf16[256,256]{1,0:T(8,128)(2,1)} %constant.9.clone.forward_ref) | copy-start | bytes 393220
  10.1 7.4 %copy-start.2 = (bf16[256,128]{1,0:T(8,128)(2,1)S(1)}, bf16[256,128]{1,0:T(8,128)(2,1)}, u32[]{:S(2)}) copy-start(bf16[256,128]{1,0:T(8,128)(2,1)} %constant.11.clone.inverse_low_ref) | copy-start | bytes 196612
  10.2 5.0 %collective-permute-start = (bf16[256,256]{1,0:T(8,128)(2,1)S(1)}, bf16[256,256]{1,0:T(8,128)(2,1)S(1)}, u32[]{:S(2)}, u32[]{:S(2)}) collective-permute-start(bf16[256,256]{1,0:T(8,128)(2,1)S(1)} %copy-done), channel_id=1, source_target_pairs={{0,2},{2,0},{1,3},{3,1},{4,6},{6,4},{5,7},{7,5},{8,10},{10,8},{9,1... | collective-permute-start | bytes 393224 | tf_op jit(solution)/shard_map/ppermute | solution.py:310
  31.7 1.4 %collective-permute-start.1 = (f32[256,128]{1,0:T(8,128)S(1)}, f32[256,128]{1,0:T(8,128)S(1)}, u32[]{:S(2)}, u32[]{:S(2)}) collective-permute-start(f32[256,128]{1,0:T(8,128)S(1)} %shard_map.139), channel_id=1, source_target_pairs={{0,1},{1,0},{2,3},{3,2},{4,5},{5,4},{6,7},{7,6},{8,9},{9,8},{10,11... | collective-permute-start | bytes 393224 | tf_op jit(solution)/shard_map/ppermute | solution.py:360

commit v5 on v4

--- a/solution.py
+++ b/solution.py
@@ -53,7 +53,11 @@
     live_hbm,
     send_hbm,
     recv_hbm,
+    filters_hbm,
+    table_hbm,
     out_ref,
+    response_ref,
+    column_ref,
     currents_ref,
     group_ref,
     projection_ref,
@@ -63,31 +67,39 @@
     live_ref,
     send_ref,
     recv_ref,
+    filters_ref,
+    table_ref,
     sems,
 ):
-    wide = [
+    moves = [
+        (filters_hbm, filters_ref),
+        (table_hbm, table_ref),
+        (group_hbm, group_ref),
+        (src_hbm, src_ref),
+        (dst_hbm, dst_ref),
+        (type_hbm, type_ref),
+        (live_hbm, live_ref),
+        (send_hbm, send_ref),
+        (recv_hbm, recv_ref),
+        (projection_hbm, projection_ref),
+        (currents_hbm, currents_ref),
+    ]
+    copies = [
         pltpu.make_async_copy(source, target, sems.at[i])
-        for i, (source, target) in enumerate(
-            [(projection_hbm, projection_ref), (currents_hbm, currents_ref), (group_hbm, group_ref)]
-        )
+        for i, (source, target) in enumerate(moves)
     ]
-    small = [
-        pltpu.make_async_copy(source, target, sems.at[len(wide) + i])
-        for i, (source, target) in enumerate(
-            [
-                (src_hbm, src_ref),
-                (dst_hbm, dst_ref),
-                (type_hbm, type_ref),
-                (live_hbm, live_ref),
-                (send_hbm, send_ref),
-                (recv_hbm, recv_ref),
-            ]
-        )
-    ]
-    for copy in wide + small:
+    for copy in copies:
         copy.start()
-
-    steps = currents_ref.shape[1]
+    for copy in copies[:3]:
+        copy.wait()
+    for c in range(filters_ref.shape[0]):
+        taps_c = filters_ref[c]
+        taps_c = jnp.concatenate([taps_c, taps_c], axis=0)
+        response_ref[c] = dot(taps_c, table_ref[...], ((0,), (0,)))
+    column_ref[...] = jnp.broadcast_to(
+        group_ref[...].astype(F32), (LANES, group_ref.shape[1])
+    ).T
+
     block = projection_ref.shape[1] // readers
     rows = out_ref.shape[1]
     me = lax.axis_index("grp")
@@ -95,7 +107,7 @@
     first = lax.rem(me, pack) * slots
     lane = lax.broadcasted_iota(jnp.int32, (TABLE_ROWS, LANES), 1)
     row = lax.broadcasted_iota(jnp.int32, (TABLE_ROWS, LANES), 0)
-    for copy in small + wide:
+    for copy in copies[3:]:
         copy.wait()
     live = live_ref[0, 0]
 
@@ -124,17 +136,6 @@
             out_ref[owner, pl.ds(g * block, block), :] = signature[
                 owner * block : (owner + 1) * block
             ]
-
-
-def filter_kernel(group_ref, filters_ref, wave_ref, out_ref, column_ref):
-    types, taps, width = filters_ref.shape
-    wave = wave_ref[...]
-    for c in range(types):
-        taps_c = filters_ref[c]
-        out_ref[c] = dot(jnp.concatenate([taps_c, taps_c], axis=0), wave, ((0,), (0,)))
-    column_ref[...] = jnp.broadcast_to(
-        group_ref[...].astype(F32), (LANES, group_ref.shape[1])
-    ).T
 
 
 def split(value):
@@ -296,32 +297,33 @@
         live_count.reshape(1, 1),
         send_group,
         recv_group,
-    )
-    outgoing = pl.pallas_call(
+        filters,
+        jnp.asarray(np.concatenate([forward_high[:taps], forward_low[:taps]], axis=0)),
+    )
+    near_table = (0, 1, 2, 9, 10)
+    partner = lax.ppermute(projection, "outer", [(0, 1), (1, 0)])
+    outgoing, response, column = pl.pallas_call(
         functools.partial(project_kernel, readers, slots),
-        out_shape=jax.ShapeDtypeStruct((readers, rows, steps), BF16),
-        in_specs=[FAR] * len(inputs),
-        out_specs=VMEM,
-        scratch_shapes=[pltpu.VMEM(x.shape, x.dtype) for x in inputs[:3]]
-        + [pltpu.SMEM(x.shape, x.dtype) for x in inputs[3:]]
-        + [pltpu.SemaphoreType.DMA((len(inputs),))],
-    )(*inputs)
-    arrived = lax.all_to_all(outgoing, "grp", split_axis=0, concat_axis=0, tiled=True)
-    partner = lax.ppermute(projection, "outer", [(0, 1), (1, 0)])
-    response, column = pl.pallas_call(
-        filter_kernel,
         out_shape=(
+            pltpu.VMEM((readers, rows, steps), BF16),
             pltpu.VMEM((types, width, 2 * steps), F32),
             pltpu.VMEM((basis, LANES), F32),
         ),
-        in_specs=[VMEM, VMEM, VMEM],
-        out_specs=(VMEM, VMEM),
+        in_specs=[FAR] * len(inputs),
+        out_specs=(VMEM, VMEM, VMEM),
         compiler_params=PARAMS,
-        cost_estimate=pl.CostEstimate(
-            flops=8 * types * width * taps * steps, bytes_accessed=2**21, transcendentals=0
-        ),
-    )(group_row, filters, np.concatenate([forward_high[:taps], forward_low[:taps]], axis=0))
-    arrived, partner = lax.optimization_barrier((arrived, partner))
+        scratch_shapes=[
+            (pltpu.VMEM if i in near_table else pltpu.SMEM)(x.shape, x.dtype)
+            for i, x in enumerate(inputs)
+        ]
+        + [pltpu.SemaphoreType.DMA((len(inputs),))],
+    )(
+        *[
+            x if x.size == 1 else pltpu.with_memory_space_constraint(x, pltpu.HBM)
+            for x in inputs
+        ]
+    )
+    arrived = lax.all_to_all(outgoing, "grp", split_axis=0, concat_axis=0, tiled=True)
     incoming = pl.pallas_call(
         functools.partial(translate_kernel, readers, slots, block),
         out_shape=pltpu.VMEM((outer * groups * block, steps), BF16),
@@ -341,6 +343,7 @@
         near(jnp.asarray(inverse_high)),
         near(jnp.asarray(inverse_low)),
     )
+    incoming, partner = lax.optimization_barrier((incoming, partner))
     incoming = incoming.reshape(outer * readers, G_DEV * block, steps)
     own = lax.all_to_all(incoming, ("outer", "grp"), split_axis=0, concat_axis=0, tiled=True)
     term = pl.pallas_call(

time: 34 us -> 34.2 us (level)
  waiting for transfers between devices: 6.87 us -> 7.22 us
    all_to_all x1, waiting for transfers between devices: 2.39 us -> 5.89 us  [local(): lax.all_to_all(outgoing, 'grp', split_axis=0, concat_axis=0, tiled=True)]
    ppermute x1, waiting for transfers between devices: 3.14 us -> 0.01 us  [local(): partner = lax.ppermute(projection, 'outer', [(0, 1), (1, 0)])]
    pallas_call x1, Pallas kernels: 1.95 us -> 2.32 us  [local(): pl.pallas_call(functools.partial(project_kernel, readers, slots), out_sha...]
  transfers between devices with their start and end apart: 3 -> 3, of which waited for: 3 -> 2; matrix products, arithmetic and copies ran while one was open for 0% -> 0% of each run, Pallas kernels for 1% -> 3%
where the time goes in v5:
time: 34.2 us; the launch traced here: 34 us
  blocking collectives  12.7 us (37%)
  starting transfers between devices  9.09 us (27%)
  waiting for transfers between devices  7.22 us (21%)
  Pallas kernels  3.5 us (10%)
  between operations  0.73 us (2%)
  other arithmetic  0.65 us (2%)
    all_to_all x1, blocking collectives, local(): lax.all_to_all(incoming, ('outer', 'grp'), split_axis=0, concat_axis=0, t...  12.7 us
    all_to_all x1, starting transfers between devices, local(): lax.all_to_all(outgoing, 'grp', split_axis=0, concat_axis=0, tiled=True)  7.45 us
    all_to_all x1, waiting for transfers between devices, local(): lax.all_to_all(outgoing, 'grp', split_axis=0, concat_axis=0, tiled=True)  5.89 us
    pallas_call x1, Pallas kernels, local(): pl.pallas_call(functools.partial(project_kernel, readers, slots), out_sha...  2.32 us
    ppermute x1, starting transfers between devices, local(): partner = lax.ppermute(projection, 'outer', [(0, 1), (1, 0)])  1.56 us
    ppermute x1, waiting for transfers between devices, local(): total = term + lax.ppermute(term, 'inner', [(0, 1), (1, 0)])  1.33 us
    pallas_call x1, Pallas kernels, local(): pl.pallas_call(functools.partial(translate_kernel, readers, slots, block)...  0.89 us
  transfers between devices with their start and end apart: 3, of which 2 were waited for; matrix products, arithmetic and copies ran while one was open for 0% of the time, Pallas kernels for 3%

profile of v5, /device:TPU:0, one launch (start us, length us, event | category | flops | bytes accessed | tf_op | source)
XLA Modules:
  0.0 34.0 jit_solution(9822092375351145030)
XLA Ops:
  0.7 0.0 copy-start.2
  0.7 0.0 copy-start.3
  0.7 2.3 %shard_map.136 = (bf16[8,72,128]{2,1,0:T(8,128)(2,1)}, f32[4,256,256]{2,1,0:T(8,128)S(1)}, f32[256,128]{1,0:T(8,128)S(1)}) custom-call(bf16[256,128]{1,0:T(8,128)(2,1)} %currents_hbm.1, s32[1,256]{1,0:T(1,128)} %bitcast.9, bf16[256,256]{1,0:T(8,128)(2,1)} %own_ref.1, s32[16]{0:T(128)} %src_hbm.1, s32[16]{0:T(128)} %dst_hbm.1, s32[16]{0:T(128)} %type_hbm.1, ...), custom_call_target="tpu_custom_call" | custom-call | tf_op jit(solution)/shard_map/pallas_call | solution.py:305
  3.0 0.0 copy-start
  3.0 0.0 copy-start.1
  3.0 7.5 %all-to-all-start = ((bf16[8,72,128]{2,1,0:T(8,128)(2,1)}), bf16[8,72,128]{2,1,0:T(8,128)(2,1)S(1)}, u32[]{:S(2)}, u32[]{:S(2)}) async-start(bf16[8,72,128]{2,1,0:T(8,128)(2,1)} %get-tuple-element.11), calls=%async_computation | async-start | bytes 294912 | tf_op jit(solution)/shard_map/all_to_all | solution.py:326
  10.5 0.0 copy-done
  10.5 1.6 %collective-permute-start = (bf16[256,256]{1,0:T(8,128)(2,1)S(1)}, bf16[256,256]{1,0:T(8,128)(2,1)S(1)}, u32[]{:S(2)}, u32[]{:S(2)}) collective-permute-start(bf16[256,256]{1,0:T(8,128)(2,1)S(1)} %copy-done), channel_id=1, source_target_pairs={{0,2},{2,0},{1,3},{3,1},{4,6},{6,4},{5,7},{7,5},{8,10},{10,8},{9,1... | collective-permute-start | bytes 393224 | tf_op jit(solution)/shard_map/ppermute | solution.py:304
  12.1 5.9 %all-to-all-done = bf16[8,72,128]{2,1,0:T(8,128)(2,1)S(1)} async-done(((bf16[8,72,128]{2,1,0:T(8,128)(2,1)}), bf16[8,72,128]{2,1,0:T(8,128)(2,1)S(1)}, u32[]{:S(2)}, u32[]{:S(2)}) %all-to-all-start) | async-done | bytes 147488 | tf_op jit(solution)/shard_map/all_to_all | solution.py:326
  17.9 0.0 copy-done.2
  17.9 0.0 copy-done.3
  17.9 0.0 copy-done.1
  18.0 0.9 %shard_map.137 = bf16[1024,128]{1,0:T(8,128)(2,1)S(1)} custom-call(bf16[576,128]{1,0:T(8,128)(2,1)S(1)} %bitcast.8, f32[4,256,256]{2,1,0:T(8,128)S(1)} %get-tuple-element.12.response_ref, bf16[256,256]{1,0:T(8,128)(2,1)S(1)} %copy-done.1, bf16[256,128]{1,0:T(8,128)(2,1)S(1)} %copy-done.2, bf16[256,128]{1,0:T(8,128)(2,1)S(1)} %copy-done.3), custom_call_target="tpu_custom_call" | custom-call | tf_op jit(solution)/shard_map/pallas_call | solution.py:327
  18.8 0.0 collective-permute-done.other_ref
  18.9 12.7 %all_to_all.10 = bf16[16,64,128]{2,1,0:T(8,128)(2,1)S(1)} all-to-all(bf16[16,64,128]{2,1,0:T(8,128)(2,1)S(1)} %bitcast.7), channel_id=1, replica_groups=mesh['grp'=8,'outer'=2,'inner'=2] {'outer','grp'}, dimensions={0} | all-to-all | bytes 524288 | tf_op jit(solution)/shard_map/all_to_all | solution.py:348
  31.6 0.3 shard_map.138
  31.9 0.1 collective-permute-start.1
  32.0 1.3 %collective-permute-done.1 = f32[256,128]{1,0:T(8,128)S(1)} collective-permute-done((f32[256,128]{1,0:T(8,128)S(1)}, f32[256,128]{1,0:T(8,128)S(1)}, u32[]{:S(2)}, u32[]{:S(2)}) %collective-permute-start.1) | collective-permute-done | bytes 131104 | tf_op jit(solution)/shard_map/ppermute | solution.py:363
  33.3 0.7 %add_convert_fusion = bf16[256,128]{1,0:T(8,128)(2,1)} fusion(f32[256,128]{1,0:T(8,128)S(1)} %shard_map.138, f32[256,128]{1,0:T(8,128)S(1)} %collective-permute-done.1), kind=kLoop, calls=%fused_computation | loop fusion | flops 65536 | bytes 327680 | tf_op jit(solution)/shard_map/convert_element_type | solution.py:364
Async XLA Ops:
  0.7 17.3 %copy-start.2 = (bf16[256,128]{1,0:T(8,128)(2,1)S(1)}, bf16[256,128]{1,0:T(8,128)(2,1)}, u32[]{:S(2)}) copy-start(bf16[256,128]{1,0:T(8,128)(2,1)} %constant.10.clone.inverse_high_ref) | copy-start | bytes 196612
  0.7 17.3 %copy-start.3 = (bf16[256,128]{1,0:T(8,128)(2,1)S(1)}, bf16[256,128]{1,0:T(8,128)(2,1)}, u32[]{:S(2)}) copy-start(bf16[256,128]{1,0:T(8,128)(2,1)} %constant.11.clone.inverse_low_ref) | copy-start | bytes 196612
  3.0 7.5 %copy-start = (bf16[256,256]{1,0:T(8,128)(2,1)S(1)}, bf16[256,256]{1,0:T(8,128)(2,1)}, u32[]{:S(2)}) copy-start(bf16[256,256]{1,0:T(8,128)(2,1)} %own_ref.1) | copy-start | bytes 393220
  3.0 14.9 %copy-start.1 = (bf16[256,256]{1,0:T(8,128)(2,1)S(1)}, bf16[256,256]{1,0:T(8,128)(2,1)}, u32[]{:S(2)}) copy-start(bf16[256,256]{1,0:T(8,128)(2,1)} %constant.9.clone.forward_ref) | copy-start | bytes 393220
  3.0 14.9 %all-to-all-start = ((bf16[8,72,128]{2,1,0:T(8,128)(2,1)}), bf16[8,72,128]{2,1,0:T(8,128)(2,1)S(1)}, u32[]{:S(2)}, u32[]{:S(2)}) async-start(bf16[8,72,128]{2,1,0:T(8,128)(2,1)} %get-tuple-element.11), calls=%async_computation | async-start | bytes 294912 | tf_op jit(solution)/shard_map/all_to_all | solution.py:326
  10.5 8.4 %collective-permute-start = (bf16[256,256]{1,0:T(8,128)(2,1)S(1)}, bf16[256,256]{1,0:T(8,128)(2,1)S(1)}, u32[]{:S(2)}, u32[]{:S(2)}) collective-permute-start(bf16[256,256]{1,0:T(8,128)(2,1)S(1)} %copy-done), channel_id=1, source_target_pairs={{0,2},{2,0},{1,3},{3,1},{4,6},{6,4},{5,7},{7,5},{8,10},{10,8},{9,1... | collective-permute-start | bytes 393224 | tf_op jit(solution)/shard_map/ppermute | solution.py:304
  31.9 1.4 %collective-permute-start.1 = (f32[256,128]{1,0:T(8,128)S(1)}, f32[256,128]{1,0:T(8,128)S(1)}, u32[]{:S(2)}, u32[]{:S(2)}) collective-permute-start(f32[256,128]{1,0:T(8,128)S(1)} %shard_map.138), channel_id=1, source_target_pairs={{0,1},{1,0},{2,3},{3,2},{4,5},{5,4},{6,7},{7,6},{8,9},{9,8},{10,11... | collective-permute-start | bytes 393224 | tf_op jit(solution)/shard_map/ppermute | solution.py:363

commit v6 on v5

--- a/solution.py
+++ b/solution.py
@@ -71,18 +71,24 @@
     table_ref,
     sems,
 ):
+    width, window = filters_hbm.shape[2], response_ref.shape[1]
+    base = lax.axis_index("grp") * (width // readers)
+    near = filters_hbm
+    if window < width:
+        start = pl.multiple_of(lax.div(base, window) * window, LANES)
+        near = filters_hbm.at[:, :, pl.ds(start, window)]
     moves = [
-        (filters_hbm, filters_ref),
-        (table_hbm, table_ref),
-        (group_hbm, group_ref),
         (src_hbm, src_ref),
         (dst_hbm, dst_ref),
         (type_hbm, type_ref),
         (live_hbm, live_ref),
         (send_hbm, send_ref),
         (recv_hbm, recv_ref),
+        (group_hbm, group_ref),
         (projection_hbm, projection_ref),
         (currents_hbm, currents_ref),
+        (table_hbm, table_ref),
+        (near, filters_ref),
     ]
     copies = [
         pltpu.make_async_copy(source, target, sems.at[i])
@@ -90,15 +96,6 @@
     ]
     for copy in copies:
         copy.start()
-    for copy in copies[:3]:
-        copy.wait()
-    for c in range(filters_ref.shape[0]):
-        taps_c = filters_ref[c]
-        taps_c = jnp.concatenate([taps_c, taps_c], axis=0)
-        response_ref[c] = dot(taps_c, table_ref[...], ((0,), (0,)))
-    column_ref[...] = jnp.broadcast_to(
-        group_ref[...].astype(F32), (LANES, group_ref.shape[1])
-    ).T
 
     block = projection_ref.shape[1] // readers
     rows = out_ref.shape[1]
@@ -107,7 +104,7 @@
     first = lax.rem(me, pack) * slots
     lane = lax.broadcasted_iota(jnp.int32, (TABLE_ROWS, LANES), 1)
     row = lax.broadcasted_iota(jnp.int32, (TABLE_ROWS, LANES), 0)
-    for copy in copies[3:]:
+    for copy in copies[:9]:
         copy.wait()
     live = live_ref[0, 0]
 
@@ -136,6 +133,15 @@
             out_ref[owner, pl.ds(g * block, block), :] = signature[
                 owner * block : (owner + 1) * block
             ]
+    column_ref[...] = jnp.broadcast_to(
+        group_ref[...].astype(F32), (LANES, group_ref.shape[1])
+    ).T
+    for copy in copies[9:]:
+        copy.wait()
+    for c in range(filters_ref.shape[0]):
+        taps_c = filters_ref[c]
+        taps_c = jnp.concatenate([taps_c, taps_c], axis=0)
+        response_ref[c] = dot(taps_c, table_ref[...], ((0,), (0,)))
 
 
 def split(value):
@@ -162,7 +168,7 @@
     steps = inverse_high_ref.shape[1]
     groups = readers * G_DEV
     rows = G_DEV * block + TABLE_ROWS
-    base = lax.axis_index("grp") * block
+    base = lax.rem(lax.axis_index("grp") * block, response_ref.shape[1])
 
     for owner in range(readers):
         part = arrived_ref[pl.ds(owner * rows, G_DEV * block), :]
@@ -301,19 +307,22 @@
         jnp.asarray(np.concatenate([forward_high[:taps], forward_low[:taps]], axis=0)),
     )
     near_table = (0, 1, 2, 9, 10)
+    window = LANES if width % LANES == 0 and LANES % block == 0 else width
     partner = lax.ppermute(projection, "outer", [(0, 1), (1, 0)])
     outgoing, response, column = pl.pallas_call(
         functools.partial(project_kernel, readers, slots),
         out_shape=(
             pltpu.VMEM((readers, rows, steps), BF16),
-            pltpu.VMEM((types, width, 2 * steps), F32),
+            pltpu.VMEM((types, window, 2 * steps), F32),
             pltpu.VMEM((basis, LANES), F32),
         ),
         in_specs=[FAR] * len(inputs),
         out_specs=(VMEM, VMEM, VMEM),
         compiler_params=PARAMS,
         scratch_shapes=[
-            (pltpu.VMEM if i in near_table else pltpu.SMEM)(x.shape, x.dtype)
+            (pltpu.VMEM if i in near_table else pltpu.SMEM)(
+                (types, taps, window) if x is filters else x.shape, x.dtype
+            )
             for i, x in enumerate(inputs)
         ]
         + [pltpu.SemaphoreType.DMA((len(inputs),))],

time: 34.2 us -> 33.9 us (level)
  no operation moved by 1% of the time
where the time goes in v6:
time: 33.9 us; the launch traced here: 33.6 us
  blocking collectives  12.8 us (38%)
  starting transfers between devices  9.08 us (27%)
  waiting for transfers between devices  7.23 us (21%)
  Pallas kernels  3.16 us (9%)
  between operations  0.73 us (2%)
  other arithmetic  0.65 us (2%)
    all_to_all x1, blocking collectives, local(): lax.all_to_all(incoming, ('outer', 'grp'), split_axis=0, concat_axis=0, t...  12.8 us
    all_to_all x1, starting transfers between devices, local(): lax.all_to_all(outgoing, 'grp', split_axis=0, concat_axis=0, tiled=True)  7.45 us
    all_to_all x1, waiting for transfers between devices, local(): lax.all_to_all(outgoing, 'grp', split_axis=0, concat_axis=0, tiled=True)  5.89 us
    pallas_call x1, Pallas kernels, local(): pl.pallas_call(functools.partial(project_kernel, readers, slots), out_sha...  1.98 us
    ppermute x1, starting transfers between devices, local(): partner = lax.ppermute(projection, 'outer', [(0, 1), (1, 0)])  1.56 us
    ppermute x1, waiting for transfers between devices, local(): total = term + lax.ppermute(term, 'inner', [(0, 1), (1, 0)])  1.33 us
    pallas_call x1, Pallas kernels, local(): pl.pallas_call(functools.partial(translate_kernel, readers, slots, block)...  0.89 us
  transfers between devices with their start and end apart: 3, of which 2 were waited for; matrix products, arithmetic and copies ran while one was open for 0% of the time, Pallas kernels for 3%

profile of v6, /device:TPU:0, one launch (start us, length us, event | category | flops | bytes accessed | tf_op | source)
XLA Modules:
  0.0 33.6 jit_solution(11778149120173051144)
XLA Ops:
  0.7 0.0 copy-start.2
  0.7 0.0 copy-start.3
  0.7 2.0 %shard_map.136 = (bf16[8,72,128]{2,1,0:T(8,128)(2,1)}, f32[4,128,256]{2,1,0:T(8,128)S(1)}, f32[256,128]{1,0:T(8,128)S(1)}) custom-call(bf16[256,128]{1,0:T(8,128)(2,1)} %currents_hbm.1, s32[1,256]{1,0:T(1,128)} %bitcast.9, bf16[256,256]{1,0:T(8,128)(2,1)} %own_ref.1, s32[16]{0:T(128)} %src_hbm.1, s32[16]{0:T(128)} %dst_hbm.1, s32[16]{0:T(128)} %type_hbm.1, ...), custom_call_target="tpu_custom_call" | custom-call | tf_op jit(solution)/shard_map/pallas_call | solution.py:312
  2.7 0.0 copy-start
  2.7 0.0 copy-start.1
  2.7 7.5 %all-to-all-start = ((bf16[8,72,128]{2,1,0:T(8,128)(2,1)}), bf16[8,72,128]{2,1,0:T(8,128)(2,1)S(1)}, u32[]{:S(2)}, u32[]{:S(2)}) async-start(bf16[8,72,128]{2,1,0:T(8,128)(2,1)} %get-tuple-element.11), calls=%async_computation | async-start | bytes 294912 | tf_op jit(solution)/shard_map/all_to_all | solution.py:335
  10.1 0.0 copy-done
  10.2 1.6 %collective-permute-start = (bf16[256,256]{1,0:T(8,128)(2,1)S(1)}, bf16[256,256]{1,0:T(8,128)(2,1)S(1)}, u32[]{:S(2)}, u32[]{:S(2)}) collective-permute-start(bf16[256,256]{1,0:T(8,128)(2,1)S(1)} %copy-done), channel_id=1, source_target_pairs={{0,2},{2,0},{1,3},{3,1},{4,6},{6,4},{5,7},{7,5},{8,10},{10,8},{9,1... | collective-permute-start | bytes 393224 | tf_op jit(solution)/shard_map/ppermute | solution.py:311
  11.7 5.9 %all-to-all-done = bf16[8,72,128]{2,1,0:T(8,128)(2,1)S(1)} async-done(((bf16[8,72,128]{2,1,0:T(8,128)(2,1)}), bf16[8,72,128]{2,1,0:T(8,128)(2,1)S(1)}, u32[]{:S(2)}, u32[]{:S(2)}) %all-to-all-start) | async-done | bytes 147488 | tf_op jit(solution)/shard_map/all_to_all | solution.py:335
  17.6 0.0 copy-done.2
  17.6 0.0 copy-done.3
  17.6 0.0 copy-done.1
  17.6 0.9 %shard_map.137 = bf16[1024,128]{1,0:T(8,128)(2,1)S(1)} custom-call(bf16[576,128]{1,0:T(8,128)(2,1)S(1)} %bitcast.8, f32[4,128,256]{2,1,0:T(8,128)S(1)} %get-tuple-element.12.response_ref, bf16[256,256]{1,0:T(8,128)(2,1)S(1)} %copy-done.1, bf16[256,128]{1,0:T(8,128)(2,1)S(1)} %copy-done.2, bf16[256,128]{1,0:T(8,128)(2,1)S(1)} %copy-done.3), custom_call_target="tpu_custom_call" | custom-call | tf_op jit(solution)/shard_map/pallas_call | solution.py:336
  18.5 0.0 collective-permute-done.other_ref
  18.5 12.8 %all_to_all.10 = bf16[16,64,128]{2,1,0:T(8,128)(2,1)S(1)} all-to-all(bf16[16,64,128]{2,1,0:T(8,128)(2,1)S(1)} %bitcast.7), channel_id=1, replica_groups=mesh['grp'=8,'outer'=2,'inner'=2] {'outer','grp'}, dimensions={0} | all-to-all | bytes 524288 | tf_op jit(solution)/shard_map/all_to_all | solution.py:357
  31.3 0.3 shard_map.138
  31.6 0.1 collective-permute-start.1
  31.6 1.3 %collective-permute-done.1 = f32[256,128]{1,0:T(8,128)S(1)} collective-permute-done((f32[256,128]{1,0:T(8,128)S(1)}, f32[256,128]{1,0:T(8,128)S(1)}, u32[]{:S(2)}, u32[]{:S(2)}) %collective-permute-start.1) | collective-permute-done | bytes 131104 | tf_op jit(solution)/shard_map/ppermute | solution.py:372
  33.0 0.7 %add_convert_fusion = bf16[256,128]{1,0:T(8,128)(2,1)} fusion(f32[256,128]{1,0:T(8,128)S(1)} %shard_map.138, f32[256,128]{1,0:T(8,128)S(1)} %collective-permute-done.1), kind=kLoop, calls=%fused_computation | loop fusion | flops 65536 | bytes 327680 | tf_op jit(solution)/shard_map/convert_element_type | solution.py:373
Async XLA Ops:
  0.7 17.0 %copy-start.2 = (bf16[256,128]{1,0:T(8,128)(2,1)S(1)}, bf16[256,128]{1,0:T(8,128)(2,1)}, u32[]{:S(2)}) copy-start(bf16[256,128]{1,0:T(8,128)(2,1)} %constant.10.clone.inverse_high_ref) | copy-start | bytes 196612
  0.7 16.9 %copy-start.3 = (bf16[256,128]{1,0:T(8,128)(2,1)S(1)}, bf16[256,128]{1,0:T(8,128)(2,1)}, u32[]{:S(2)}) copy-start(bf16[256,128]{1,0:T(8,128)(2,1)} %constant.11.clone.inverse_low_ref) | copy-start | bytes 196612
  2.7 7.5 %copy-start = (bf16[256,256]{1,0:T(8,128)(2,1)S(1)}, bf16[256,256]{1,0:T(8,128)(2,1)}, u32[]{:S(2)}) copy-start(bf16[256,256]{1,0:T(8,128)(2,1)} %own_ref.1) | copy-start | bytes 393220
  2.7 14.9 %copy-start.1 = (bf16[256,256]{1,0:T(8,128)(2,1)S(1)}, bf16[256,256]{1,0:T(8,128)(2,1)}, u32[]{:S(2)}) copy-start(bf16[256,256]{1,0:T(8,128)(2,1)} %constant.9.clone.forward_ref) | copy-start | bytes 393220
  2.7 14.9 %all-to-all-start = ((bf16[8,72,128]{2,1,0:T(8,128)(2,1)}), bf16[8,72,128]{2,1,0:T(8,128)(2,1)S(1)}, u32[]{:S(2)}, u32[]{:S(2)}) async-start(bf16[8,72,128]{2,1,0:T(8,128)(2,1)} %get-tuple-element.11), calls=%async_computation | async-start | bytes 294912 | tf_op jit(solution)/shard_map/all_to_all | solution.py:335
  10.2 8.4 %collective-permute-start = (bf16[256,256]{1,0:T(8,128)(2,1)S(1)}, bf16[256,256]{1,0:T(8,128)(2,1)S(1)}, u32[]{:S(2)}, u32[]{:S(2)}) collective-permute-start(bf16[256,256]{1,0:T(8,128)(2,1)S(1)} %copy-done), channel_id=1, source_target_pairs={{0,2},{2,0},{1,3},{3,1},{4,6},{6,4},{5,7},{7,5},{8,10},{10,8},{9,1... | collective-permute-start | bytes 393224 | tf_op jit(solution)/shard_map/ppermute | solution.py:311
  31.6 1.4 %collective-permute-start.1 = (f32[256,128]{1,0:T(8,128)S(1)}, f32[256,128]{1,0:T(8,128)S(1)}, u32[]{:S(2)}, u32[]{:S(2)}) collective-permute-start(f32[256,128]{1,0:T(8,128)S(1)} %shard_map.138), channel_id=1, source_target_pairs={{0,1},{1,0},{2,3},{3,2},{4,5},{5,4},{6,7},{7,6},{8,9},{9,8},{10,11... | collective-permute-start | bytes 393224 | tf_op jit(solution)/shard_map/ppermute | solution.py:372
